TPU v7x, 256 devices: a whole 4x4x8 slice. The times are simulated.
256 devices in a mesh: term: 16 (over y_lo, z), sector: 16 (over y_hi, x, core).
Axes of the slice: x: 4, y: 4 (y_hi: 2, y_lo: 2; y = y_hi * 2 + y_lo), z: 8, core: 2. Of those that a mesh axis runs over, the one named last changes fastest.
Arguments:
- wavefunction: bfloat16 [4096, 128, 128], P(('term', 'sector')), may hold values from -6 to 6
- left_sector: int32 [4096, 1], P(('term', 'sector')), may hold values from 0 to 15; in each aligned block of 16 rows (0 to 15, 16 to 31, ...) at most 2 rows name the same one
- right_sector: int32 [4096], P(('term', 'sector')), may hold values from 0 to 3
- left_blocks: bfloat16 [32, 16, 128, 128], P('term', 'sector'), may hold values from -0.5 to 0.5
- right_blocks: bfloat16 [32, 4, 128, 128], P('term'), may hold values from -0.09375 to 0.09375
Outputs:
- product_blocks: bfloat16 [4096, 128, 128], P(('term', 'sector'))
Inputs may be any that keep to these rules, and one draw needn't show every extreme that they name: `left_sector`: among the 16 blocks of one device no left sector is named more than 2 times, and some left sector is named exactly 2 times.
All inputs are finite; a program needn't handle non-finite values.
Results may differ from a plain program's by a relative error of at most 0.0049.
Values may be sent and summed in bfloat16 or wider, within the bound.
A program may use at most 64 MiB of HBM per device.

v0:
```python
import jax
import jax.numpy as jnp
from jax import lax
from jax.sharding import PartitionSpec as P


def from_behind(block, axis, distance):
    devices = range(lax.axis_size(axis))
    route = [((i - distance) % len(devices), i) for i in devices]
    return lax.ppermute(block, axis, route)


def apply_terms(summed, slot_wave, slot_right, left_now, right_now):
    for index_term in range(left_now.shape[0]):
        mixed_left = jnp.einsum(
            "ab,kbc->kac", left_now[index_term], slot_wave, preferred_element_type=jnp.float32
        ).astype(jnp.bfloat16)
        chosen = jnp.take(right_now[index_term], slot_right, axis=0)
        summed = summed + jnp.einsum(
            "kac,kdc->kad", mixed_left, chosen, preferred_element_type=jnp.float32
        )
    return summed


def local(wavefunction, left_sector, right_sector, left_blocks, right_blocks):
    n_sec = lax.axis_size("sector")
    n_term = lax.axis_size("term")
    held = wavefunction.shape[0]
    order = wavefunction.shape[1]
    capacity = max(2, 2 * held // n_sec)
    owners = left_sector[:, 0]
    onehot = (owners[:, None] == jnp.arange(n_sec, dtype=jnp.int32)[None, :]).astype(jnp.int32)
    before = jnp.cumsum(onehot, axis=0) - onehot
    slot_of = jnp.sum(before * onehot, axis=1)
    target = owners * capacity + slot_of
    slot_ids = jnp.arange(n_sec * capacity, dtype=jnp.int32)
    matched = target[None, :] == slot_ids[:, None]
    source = jnp.sum(jnp.where(matched, jnp.arange(held, dtype=jnp.int32)[None, :], 0), axis=1)
    filled = jnp.any(matched, axis=1)
    sent_wave = jnp.where(
        filled[:, None, None],
        jnp.take(wavefunction, source, axis=0),
        jnp.zeros((), wavefunction.dtype),
    )
    sent_right = jnp.where(filled, jnp.take(right_sector, source, axis=0), 0)
    got_wave, got_right = (
        lax.all_to_all(
            sent_wave.reshape(n_sec, capacity, order, order),
            "sector",
            split_axis=0,
            concat_axis=0,
            tiled=True,
        ),
        lax.all_to_all(
            sent_right.reshape(n_sec, capacity), "sector", split_axis=0, concat_axis=0, tiled=True
        ),
    )
    slot_wave = got_wave.reshape(n_sec * capacity, order, order)
    slot_right = got_right.reshape(n_sec * capacity)
    left_own = left_blocks[:, 0]
    summed = apply_terms(
        jnp.zeros((n_sec * capacity, order, order), jnp.float32),
        slot_wave,
        slot_right,
        left_own,
        right_blocks,
    )

    def advance(turn_index, carried):
        summed_now, left_now, right_now = carried
        left_now, right_now = from_behind((left_now, right_now), "term", 1)
        return (
            apply_terms(summed_now, slot_wave, slot_right, left_now, right_now),
            left_now,
            right_now,
        )

    summed, _, _ = lax.fori_loop(0, n_term - 1, advance, (summed, left_own, right_blocks))
    out_slots = summed.astype(jnp.bfloat16).reshape(n_sec, capacity, order, order)
    returned = lax.all_to_all(out_slots, "sector", split_axis=0, concat_axis=0, tiled=True)
    return jnp.take(returned.reshape(n_sec * capacity, order, order), target, axis=0)


def solution(mesh):
    placed = (
        P(("term", "sector"), None, None),
        P(("term", "sector"), None),
        P(("term", "sector")),
        P("term", "sector", None, None),
        P("term", None, None, None),
    )
    return jax.shard_map(
        local,
        mesh=mesh,
        in_specs=placed,
        out_specs=P(("term", "sector"), None, None),
        check_vma=False,
    )
```

profile of v0, /device:TPU:1, one launch (start us, length us, event | category | flops | bytes accessed | tf_op | source)
XLA Modules:
  0.0 388.8 jit_solution(17061278720347573515)
XLA Ops:
  6.6 8.4 %all-to-all-start.1 = ((s32[16,1,2]{2,1,0:T(1,128)}), s32[16,1,2]{2,1,0:T(1,128)S(1)}, u32[]{:S(2)}, u32[]{:S(2)}) async-start(s32[16,1,2]{2,1,0:T(1,128)} %bitcast.15), calls=%async_computation.1 | async-start | bytes 16384 | tf_op jit(solution)/shard_map/all_to_all | solution.py:54
  17.8 4.1 %all-to-all-done.1 = s32[16,1,2]{2,1,0:T(1,128)S(1)} async-done(((s32[16,1,2]{2,1,0:T(1,128)}), s32[16,1,2]{2,1,0:T(1,128)S(1)}, u32[]{:S(2)}, u32[]{:S(2)}) %all-to-all-start.1) | async-done | bytes 160 | tf_op jit(solution)/shard_map/all_to_all | solution.py:54
  21.9 4.7 %all-to-all-start = ((bf16[16,2,128,128]{2,3,1,0:T(8,128)(2,1)}), bf16[16,2,128,128]{2,3,1,0:T(8,128)(2,1)}, u32[]{:S(2)}, u32[]{:S(2)}) async-start(bf16[16,2,128,128]{2,3,1,0:T(8,128)(2,1)} %select_select_fusion), calls=%async_computation | async-start | bytes 2097152 | tf_op jit(solution)/shard_map/all_to_all | solution.py:47
  28.0 1.7 gather_fusion.5
  29.7 1.7 gather_fusion.6
  31.4 12.8 %all-to-all-done = bf16[16,2,128,128]{2,3,1,0:T(8,128)(2,1)} async-done(((bf16[16,2,128,128]{2,3,1,0:T(8,128)(2,1)}), bf16[16,2,128,128]{2,3,1,0:T(8,128)(2,1)}, u32[]{:S(2)}, u32[]{:S(2)}) %all-to-all-start) | async-done | bytes 1048608 | tf_op jit(solution)/shard_map/all_to_all | solution.py:47
  44.1 2.8 fusion.9
  46.9 4.2 %convolution_add_fusion = f32[32,128,128]{2,1,0:T(8,128)} fusion(f32[32,128,128]{2,1,0:T(8,128)S(1)} %fusion.9, bf16[32,128,128]{1,2,0:T(8,128)(2,1)} %bitcast.12, bf16[32,128,128]{2,1,0:T(8,128)(2,1)} %gather_fusion.6, pred[32]{0:T(512)(128)(4,1)S(1)} %compare_and_fusion.2, bf16[2,1,128,128]{3,2,1,0:T(8,128)(2,1)S(1)} %copy.37), kind=kOutput, calls=%fused_computation.26 | convolution fusion | flops 270008320 | bytes 6324736 | tf_op jit(solution)/shard_map/kac,kdc->kad/dot_general | solution.py:19
  51.1 293.9 %while.14 = (s32[]{:T(128)}, f32[32,128,128]{2,1,0:T(8,128)}, bf16[2,128,128]{2,1,0:T(8,128)(2,1)S(1)}, bf16[2,4,128,128]{3,2,1,0:T(8,128)(2,1)S(1)}, bf16[32,12...) while((s32[]{:T(128)}, f32[32,128,128]{2,1,0:T(8,128)}, bf16[2,128,128]{2,1,0:T(8,128)(2,1)S(1)}, ...), condition=%wide.region_5.7_spmd, body=%wide.region_4.6_spmd.sunk | while | flops 540017920 | bytes 19339196 | solution.py:78
  54.4 9.7 %collective-permute-done.1 = bf16[2,128,128]{2,1,0:T(8,128)(2,1)S(1)} collective-permute-done((bf16[2,128,128]{2,1,0:T(8,128)(2,1)S(1)}, bf16[2,128,128]{2,1,0:T(8,128)(2,1)S(1)}, u32[]{:S(2)}, u32[]{:S(2)}) %collective-permute-start.1) | collective-permute-done | bytes 65568 | tf_op jit(solution)/shard_map/while/body/eval_jaxpr/ppermute | solution.py:10
  65.8 1.7 gather_fusion.1
  67.5 2.8 fusion.42
  70.3 4.8 %add_add_fusion.2 = f32[32,128,128]{2,1,0:T(8,128)} fusion(f32[32,128,128]{2,1,0:T(8,128)} %get-tuple-element.106, f32[32,128,128]{2,1,0:T(8,128)S(1)} %fusion.42, bf16[32,128,128]{1,2,0:T(8,128)(2,1)} %get-tuple-element.116, bf16[32,128,128]{2,1,0:T(8,128)(2,1)} %gather_fusion.1, pred[32]{0:T(512)(128)(4,1)S(1)} %compare_and_fusion.4, ...), kind=kOutput, calls=%fused_computation.7.clone.1 | convolution fusion | flops 270532608 | bytes 8421888 | tf_op jit(solution)/shard_map/while/body/eval_jaxpr/kac,kdc->kad/dot_general | solution.py:19
  75.1 10.0 %collective-permute-done.1 = bf16[2,128,128]{2,1,0:T(8,128)(2,1)S(1)} collective-permute-done((bf16[2,128,128]{2,1,0:T(8,128)(2,1)S(1)}, bf16[2,128,128]{2,1,0:T(8,128)(2,1)S(1)}, u32[]{:S(2)}, u32[]{:S(2)}) %collective-permute-start.1) | collective-permute-done | bytes 65568 | tf_op jit(solution)/shard_map/while/body/eval_jaxpr/ppermute | solution.py:10
  86.8 1.7 gather_fusion.1
  88.5 2.8 fusion.42
  91.3 4.8 %add_add_fusion.2 = f32[32,128,128]{2,1,0:T(8,128)} fusion(f32[32,128,128]{2,1,0:T(8,128)} %get-tuple-element.106, f32[32,128,128]{2,1,0:T(8,128)S(1)} %fusion.42, bf16[32,128,128]{1,2,0:T(8,128)(2,1)} %get-tuple-element.116, bf16[32,128,128]{2,1,0:T(8,128)(2,1)} %gather_fusion.1, pred[32]{0:T(512)(128)(4,1)S(1)} %compare_and_fusion.4, ...), kind=kOutput, calls=%fused_computation.7.clone.1 | convolution fusion | flops 270532608 | bytes 8421888 | tf_op jit(solution)/shard_map/while/body/eval_jaxpr/kac,kdc->kad/dot_general | solution.py:19
  96.2 9.1 %collective-permute-done.1 = bf16[2,128,128]{2,1,0:T(8,128)(2,1)S(1)} collective-permute-done((bf16[2,128,128]{2,1,0:T(8,128)(2,1)S(1)}, bf16[2,128,128]{2,1,0:T(8,128)(2,1)S(1)}, u32[]{:S(2)}, u32[]{:S(2)}) %collective-permute-start.1) | collective-permute-done | bytes 65568 | tf_op jit(solution)/shard_map/while/body/eval_jaxpr/ppermute | solution.py:10
  107.0 1.7 gather_fusion.1
  108.7 2.8 fusion.42
  111.5 4.8 %add_add_fusion.2 = f32[32,128,128]{2,1,0:T(8,128)} fusion(f32[32,128,128]{2,1,0:T(8,128)} %get-tuple-element.106, f32[32,128,128]{2,1,0:T(8,128)S(1)} %fusion.42, bf16[32,128,128]{1,2,0:T(8,128)(2,1)} %get-tuple-element.116, bf16[32,128,128]{2,1,0:T(8,128)(2,1)} %gather_fusion.1, pred[32]{0:T(512)(128)(4,1)S(1)} %compare_and_fusion.4, ...), kind=kOutput, calls=%fused_computation.7.clone.1 | convolution fusion | flops 270532608 | bytes 8421888 | tf_op jit(solution)/shard_map/while/body/eval_jaxpr/kac,kdc->kad/dot_general | solution.py:19
  116.4 8.0 %collective-permute-done.1 = bf16[2,128,128]{2,1,0:T(8,128)(2,1)S(1)} collective-permute-done((bf16[2,128,128]{2,1,0:T(8,128)(2,1)S(1)}, bf16[2,128,128]{2,1,0:T(8,128)(2,1)S(1)}, u32[]{:S(2)}, u32[]{:S(2)}) %collective-permute-start.1) | collective-permute-done | bytes 65568 | tf_op jit(solution)/shard_map/while/body/eval_jaxpr/ppermute | solution.py:10
  126.1 1.7 gather_fusion.1
  127.7 2.8 fusion.42
  130.5 4.8 %add_add_fusion.2 = f32[32,128,128]{2,1,0:T(8,128)} fusion(f32[32,128,128]{2,1,0:T(8,128)} %get-tuple-element.106, f32[32,128,128]{2,1,0:T(8,128)S(1)} %fusion.42, bf16[32,128,128]{1,2,0:T(8,128)(2,1)} %get-tuple-element.116, bf16[32,128,128]{2,1,0:T(8,128)(2,1)} %gather_fusion.1, pred[32]{0:T(512)(128)(4,1)S(1)} %compare_and_fusion.4, ...), kind=kOutput, calls=%fused_computation.7.clone.1 | convolution fusion | flops 270532608 | bytes 8421888 | tf_op jit(solution)/shard_map/while/body/eval_jaxpr/kac,kdc->kad/dot_general | solution.py:19
  135.4 8.0 %collective-permute-done.1 = bf16[2,128,128]{2,1,0:T(8,128)(2,1)S(1)} collective-permute-done((bf16[2,128,128]{2,1,0:T(8,128)(2,1)S(1)}, bf16[2,128,128]{2,1,0:T(8,128)(2,1)S(1)}, u32[]{:S(2)}, u32[]{:S(2)}) %collective-permute-start.1) | collective-permute-done | bytes 65568 | tf_op jit(solution)/shard_map/while/body/eval_jaxpr/ppermute | solution.py:10
  145.1 1.7 gather_fusion.1
  146.8 2.8 fusion.42
  149.6 4.8 %add_add_fusion.2 = f32[32,128,128]{2,1,0:T(8,128)} fusion(f32[32,128,128]{2,1,0:T(8,128)} %get-tuple-element.106, f32[32,128,128]{2,1,0:T(8,128)S(1)} %fusion.42, bf16[32,128,128]{1,2,0:T(8,128)(2,1)} %get-tuple-element.116, bf16[32,128,128]{2,1,0:T(8,128)(2,1)} %gather_fusion.1, pred[32]{0:T(512)(128)(4,1)S(1)} %compare_and_fusion.4, ...), kind=kOutput, calls=%fused_computation.7.clone.1 | convolution fusion | flops 270532608 | bytes 8421888 | tf_op jit(solution)/shard_map/while/body/eval_jaxpr/kac,kdc->kad/dot_general | solution.py:19
  154.5 8.0 %collective-permute-done.1 = bf16[2,128,128]{2,1,0:T(8,128)(2,1)S(1)} collective-permute-done((bf16[2,128,128]{2,1,0:T(8,128)(2,1)S(1)}, bf16[2,128,128]{2,1,0:T(8,128)(2,1)S(1)}, u32[]{:S(2)}, u32[]{:S(2)}) %collective-permute-start.1) | collective-permute-done | bytes 65568 | tf_op jit(solution)/shard_map/while/body/eval_jaxpr/ppermute | solution.py:10
  164.2 1.7 gather_fusion.1
  165.8 2.8 fusion.42
  168.6 4.8 %add_add_fusion.2 = f32[32,128,128]{2,1,0:T(8,128)} fusion(f32[32,128,128]{2,1,0:T(8,128)} %get-tuple-element.106, f32[32,128,128]{2,1,0:T(8,128)S(1)} %fusion.42, bf16[32,128,128]{1,2,0:T(8,128)(2,1)} %get-tuple-element.116, bf16[32,128,128]{2,1,0:T(8,128)(2,1)} %gather_fusion.1, pred[32]{0:T(512)(128)(4,1)S(1)} %compare_and_fusion.4, ...), kind=kOutput, calls=%fused_computation.7.clone.1 | convolution fusion | flops 270532608 | bytes 8421888 | tf_op jit(solution)/shard_map/while/body/eval_jaxpr/kac,kdc->kad/dot_general | solution.py:19
  173.5 8.0 %collective-permute-done.1 = bf16[2,128,128]{2,1,0:T(8,128)(2,1)S(1)} collective-permute-done((bf16[2,128,128]{2,1,0:T(8,128)(2,1)S(1)}, bf16[2,128,128]{2,1,0:T(8,128)(2,1)S(1)}, u32[]{:S(2)}, u32[]{:S(2)}) %collective-permute-start.1) | collective-permute-done | bytes 65568 | tf_op jit(solution)/shard_map/while/body/eval_jaxpr/ppermute | solution.py:10
  183.2 1.7 gather_fusion.1
  184.9 2.8 fusion.42
  187.7 4.8 %add_add_fusion.2 = f32[32,128,128]{2,1,0:T(8,128)} fusion(f32[32,128,128]{2,1,0:T(8,128)} %get-tuple-element.106, f32[32,128,128]{2,1,0:T(8,128)S(1)} %fusion.42, bf16[32,128,128]{1,2,0:T(8,128)(2,1)} %get-tuple-element.116, bf16[32,128,128]{2,1,0:T(8,128)(2,1)} %gather_fusion.1, pred[32]{0:T(512)(128)(4,1)S(1)} %compare_and_fusion.4, ...), kind=kOutput, calls=%fused_computation.7.clone.1 | convolution fusion | flops 270532608 | bytes 8421888 | tf_op jit(solution)/shard_map/while/body/eval_jaxpr/kac,kdc->kad/dot_general | solution.py:19
  192.6 8.0 %collective-permute-done.1 = bf16[2,128,128]{2,1,0:T(8,128)(2,1)S(1)} collective-permute-done((bf16[2,128,128]{2,1,0:T(8,128)(2,1)S(1)}, bf16[2,128,128]{2,1,0:T(8,128)(2,1)S(1)}, u32[]{:S(2)}, u32[]{:S(2)}) %collective-permute-start.1) | collective-permute-done | bytes 65568 | tf_op jit(solution)/shard_map/while/body/eval_jaxpr/ppermute | solution.py:10
  203.9 2.8 fusion.42
  206.7 4.8 %add_add_fusion.2 = f32[32,128,128]{2,1,0:T(8,128)} fusion(f32[32,128,128]{2,1,0:T(8,128)} %get-tuple-element.106, f32[32,128,128]{2,1,0:T(8,128)S(1)} %fusion.42, bf16[32,128,128]{1,2,0:T(8,128)(2,1)} %get-tuple-element.116, bf16[32,128,128]{2,1,0:T(8,128)(2,1)} %gather_fusion.1, pred[32]{0:T(512)(128)(4,1)S(1)} %compare_and_fusion.4, ...), kind=kOutput, calls=%fused_computation.7.clone.1 | convolution fusion | flops 270532608 | bytes 8421888 | tf_op jit(solution)/shard_map/while/body/eval_jaxpr/kac,kdc->kad/dot_general | solution.py:19
  211.6 8.0 %collective-permute-done.1 = bf16[2,128,128]{2,1,0:T(8,128)(2,1)S(1)} collective-permute-done((bf16[2,128,128]{2,1,0:T(8,128)(2,1)S(1)}, bf16[2,128,128]{2,1,0:T(8,128)(2,1)S(1)}, u32[]{:S(2)}, u32[]{:S(2)}) %collective-permute-start.1) | collective-permute-done | bytes 65568 | tf_op jit(solution)/shard_map/while/body/eval_jaxpr/ppermute | solution.py:10
  223.0 2.8 fusion.42
  225.8 4.8 %add_add_fusion.2 = f32[32,128,128]{2,1,0:T(8,128)} fusion(f32[32,128,128]{2,1,0:T(8,128)} %get-tuple-element.106, f32[32,128,128]{2,1,0:T(8,128)S(1)} %fusion.42, bf16[32,128,128]{1,2,0:T(8,128)(2,1)} %get-tuple-element.116, bf16[32,128,128]{2,1,0:T(8,128)(2,1)} %gather_fusion.1, pred[32]{0:T(512)(128)(4,1)S(1)} %compare_and_fusion.4, ...), kind=kOutput, calls=%fused_computation.7.clone.1 | convolution fusion | flops 270532608 | bytes 8421888 | tf_op jit(solution)/shard_map/while/body/eval_jaxpr/kac,kdc->kad/dot_general | solution.py:19
  230.7 8.0 %collective-permute-done.1 = bf16[2,128,128]{2,1,0:T(8,128)(2,1)S(1)} collective-permute-done((bf16[2,128,128]{2,1,0:T(8,128)(2,1)S(1)}, bf16[2,128,128]{2,1,0:T(8,128)(2,1)S(1)}, u32[]{:S(2)}, u32[]{:S(2)}) %collective-permute-start.1) | collective-permute-done | bytes 65568 | tf_op jit(solution)/shard_map/while/body/eval_jaxpr/ppermute | solution.py:10
  242.0 2.8 fusion.42
  244.8 4.8 %add_add_fusion.2 = f32[32,128,128]{2,1,0:T(8,128)} fusion(f32[32,128,128]{2,1,0:T(8,128)} %get-tuple-element.106, f32[32,128,128]{2,1,0:T(8,128)S(1)} %fusion.42, bf16[32,128,128]{1,2,0:T(8,128)(2,1)} %get-tuple-element.116, bf16[32,128,128]{2,1,0:T(8,128)(2,1)} %gather_fusion.1, pred[32]{0:T(512)(128)(4,1)S(1)} %compare_and_fusion.4, ...), kind=kOutput, calls=%fused_computation.7.clone.1 | convolution fusion | flops 270532608 | bytes 8421888 | tf_op jit(solution)/shard_map/while/body/eval_jaxpr/kac,kdc->kad/dot_general | solution.py:19
  249.7 8.0 %collective-permute-done.1 = bf16[2,128,128]{2,1,0:T(8,128)(2,1)S(1)} collective-permute-done((bf16[2,128,128]{2,1,0:T(8,128)(2,1)S(1)}, bf16[2,128,128]{2,1,0:T(8,128)(2,1)S(1)}, u32[]{:S(2)}, u32[]{:S(2)}) %collective-permute-start.1) | collective-permute-done | bytes 65568 | tf_op jit(solution)/shard_map/while/body/eval_jaxpr/ppermute | solution.py:10
  261.1 2.8 fusion.42
  263.9 4.8 %add_add_fusion.2 = f32[32,128,128]{2,1,0:T(8,128)} fusion(f32[32,128,128]{2,1,0:T(8,128)} %get-tuple-element.106, f32[32,128,128]{2,1,0:T(8,128)S(1)} %fusion.42, bf16[32,128,128]{1,2,0:T(8,128)(2,1)} %get-tuple-element.116, bf16[32,128,128]{2,1,0:T(8,128)(2,1)} %gather_fusion.1, pred[32]{0:T(512)(128)(4,1)S(1)} %compare_and_fusion.4, ...), kind=kOutput, calls=%fused_computation.7.clone.1 | convolution fusion | flops 270532608 | bytes 8421888 | tf_op jit(solution)/shard_map/while/body/eval_jaxpr/kac,kdc->kad/dot_general | solution.py:19
  268.8 8.0 %collective-permute-done.1 = bf16[2,128,128]{2,1,0:T(8,128)(2,1)S(1)} collective-permute-done((bf16[2,128,128]{2,1,0:T(8,128)(2,1)S(1)}, bf16[2,128,128]{2,1,0:T(8,128)(2,1)S(1)}, u32[]{:S(2)}, u32[]{:S(2)}) %collective-permute-start.1) | collective-permute-done | bytes 65568 | tf_op jit(solution)/shard_map/while/body/eval_jaxpr/ppermute | solution.py:10
  280.1 2.8 fusion.42
  282.9 4.8 %add_add_fusion.2 = f32[32,128,128]{2,1,0:T(8,128)} fusion(f32[32,128,128]{2,1,0:T(8,128)} %get-tuple-element.106, f32[32,128,128]{2,1,0:T(8,128)S(1)} %fusion.42, bf16[32,128,128]{1,2,0:T(8,128)(2,1)} %get-tuple-element.116, bf16[32,128,128]{2,1,0:T(8,128)(2,1)} %gather_fusion.1, pred[32]{0:T(512)(128)(4,1)S(1)} %compare_and_fusion.4, ...), kind=kOutput, calls=%fused_computation.7.clone.1 | convolution fusion | flops 270532608 | bytes 8421888 | tf_op jit(solution)/shard_map/while/body/eval_jaxpr/kac,kdc->kad/dot_general | solution.py:19
  287.8 8.0 %collective-permute-done.1 = bf16[2,128,128]{2,1,0:T(8,128)(2,1)S(1)} collective-permute-done((bf16[2,128,128]{2,1,0:T(8,128)(2,1)S(1)}, bf16[2,128,128]{2,1,0:T(8,128)(2,1)S(1)}, u32[]{:S(2)}, u32[]{:S(2)}) %collective-permute-start.1) | collective-permute-done | bytes 65568 | tf_op jit(solution)/shard_map/while/body/eval_jaxpr/ppermute | solution.py:10
  299.2 2.8 fusion.42
  302.0 4.8 %add_add_fusion.2 = f32[32,128,128]{2,1,0:T(8,128)} fusion(f32[32,128,128]{2,1,0:T(8,128)} %get-tuple-element.106, f32[32,128,128]{2,1,0:T(8,128)S(1)} %fusion.42, bf16[32,128,128]{1,2,0:T(8,128)(2,1)} %get-tuple-element.116, bf16[32,128,128]{2,1,0:T(8,128)(2,1)} %gather_fusion.1, pred[32]{0:T(512)(128)(4,1)S(1)} %compare_and_fusion.4, ...), kind=kOutput, calls=%fused_computation.7.clone.1 | convolution fusion | flops 270532608 | bytes 8421888 | tf_op jit(solution)/shard_map/while/body/eval_jaxpr/kac,kdc->kad/dot_general | solution.py:19
  306.9 8.0 %collective-permute-done.1 = bf16[2,128,128]{2,1,0:T(8,128)(2,1)S(1)} collective-permute-done((bf16[2,128,128]{2,1,0:T(8,128)(2,1)S(1)}, bf16[2,128,128]{2,1,0:T(8,128)(2,1)S(1)}, u32[]{:S(2)}, u32[]{:S(2)}) %collective-permute-start.1) | collective-permute-done | bytes 65568 | tf_op jit(solution)/shard_map/while/body/eval_jaxpr/ppermute | solution.py:10
  318.3 2.8 fusion.42
  321.0 4.8 %add_add_fusion.2 = f32[32,128,128]{2,1,0:T(8,128)} fusion(f32[32,128,128]{2,1,0:T(8,128)} %get-tuple-element.106, f32[32,128,128]{2,1,0:T(8,128)S(1)} %fusion.42, bf16[32,128,128]{1,2,0:T(8,128)(2,1)} %get-tuple-element.116, bf16[32,128,128]{2,1,0:T(8,128)(2,1)} %gather_fusion.1, pred[32]{0:T(512)(128)(4,1)S(1)} %compare_and_fusion.4, ...), kind=kOutput, calls=%fused_computation.7.clone.1 | convolution fusion | flops 270532608 | bytes 8421888 | tf_op jit(solution)/shard_map/while/body/eval_jaxpr/kac,kdc->kad/dot_general | solution.py:19
  325.9 8.0 %collective-permute-done.1 = bf16[2,128,128]{2,1,0:T(8,128)(2,1)S(1)} collective-permute-done((bf16[2,128,128]{2,1,0:T(8,128)(2,1)S(1)}, bf16[2,128,128]{2,1,0:T(8,128)(2,1)S(1)}, u32[]{:S(2)}, u32[]{:S(2)}) %collective-permute-start.1) | collective-permute-done | bytes 65568 | tf_op jit(solution)/shard_map/while/body/eval_jaxpr/ppermute | solution.py:10
  337.3 2.8 fusion.42
  340.1 4.8 %add_add_fusion.2 = f32[32,128,128]{2,1,0:T(8,128)} fusion(f32[32,128,128]{2,1,0:T(8,128)} %get-tuple-element.106, f32[32,128,128]{2,1,0:T(8,128)S(1)} %fusion.42, bf16[32,128,128]{1,2,0:T(8,128)(2,1)} %get-tuple-element.116, bf16[32,128,128]{2,1,0:T(8,128)(2,1)} %gather_fusion.1, pred[32]{0:T(512)(128)(4,1)S(1)} %compare_and_fusion.4, ...), kind=kOutput, calls=%fused_computation.7.clone.1 | convolution fusion | flops 270532608 | bytes 8421888 | tf_op jit(solution)/shard_map/while/body/eval_jaxpr/kac,kdc->kad/dot_general | solution.py:19
  344.9 2.8 convert_element_type.25
  347.7 22.3 %all-to-all-start.2 = ((bf16[16,2,128,128]{3,2,1,0:T(8,128)(2,1)}), bf16[16,2,128,128]{3,2,1,0:T(8,128)(2,1)S(1)}, u32[]{:S(2)}, u32[]{:S(2)}) async-start(bf16[16,2,128,128]{3,2,1,0:T(8,128)(2,1)} %bitcast.21), calls=%async_computation.2 | async-start | bytes 2097152 | tf_op jit(solution)/shard_map/all_to_all | solution.py:80
  370.0 17.2 %all-to-all-done.2 = bf16[16,2,128,128]{3,2,1,0:T(8,128)(2,1)S(1)} async-done(((bf16[16,2,128,128]{3,2,1,0:T(8,128)(2,1)}), bf16[16,2,128,128]{3,2,1,0:T(8,128)(2,1)S(1)}, u32[]{:S(2)}, u32[]{:S(2)}) %all-to-all-start.2) | async-done | bytes 1048608 | tf_op jit(solution)/shard_map/all_to_all | solution.py:80
  (194 shorter events, 54.6 us)
Async XLA Ops:
  0.0 15.2 %copy-start = (bf16[16,128,128]{2,1,0:T(8,128)(2,1)S(1)}, bf16[16,128,128]{2,1,0:T(8,128)(2,1)}, u32[]{:S(2)}) copy-start(bf16[16,128,128]{2,1,0:T(8,128)(2,1)} %param.9) | copy-start | bytes 1572868
  6.6 15.4 %all-to-all-start.1 = ((s32[16,1,2]{2,1,0:T(1,128)}), s32[16,1,2]{2,1,0:T(1,128)S(1)}, u32[]{:S(2)}, u32[]{:S(2)}) async-start(s32[16,1,2]{2,1,0:T(1,128)} %bitcast.15), calls=%async_computation.1 | async-start | bytes 16384 | tf_op jit(solution)/shard_map/all_to_all | solution.py:54
  21.9 22.2 %all-to-all-start = ((bf16[16,2,128,128]{2,3,1,0:T(8,128)(2,1)}), bf16[16,2,128,128]{2,3,1,0:T(8,128)(2,1)}, u32[]{:S(2)}, u32[]{:S(2)}) async-start(bf16[16,2,128,128]{2,3,1,0:T(8,128)(2,1)} %select_select_fusion), calls=%async_computation | async-start | bytes 2097152 | tf_op jit(solution)/shard_map/all_to_all | solution.py:47
  51.1 13.0 %collective-permute-start = (bf16[2,4,128,128]{3,2,1,0:T(8,128)(2,1)S(1)}, bf16[2,4,128,128]{3,2,1,0:T(8,128)(2,1)S(1)}, u32[]{:S(2)}, u32[]{:S(2)}) collective-permute-start(bf16[2,4,128,128]{3,2,1,0:T(8,128)(2,1)S(1)} %get-tuple-element.108), channel_id=1, source_target_pairs={{240,0},{0,16},{16,32},{32,48},{48,64},{64,80},{80,96},{96,112},{1... | collective-permute-start | bytes 786440 | tf_op jit(solution)/shard_map/while/body/eval_jaxpr/ppermute | solution.py:10
  52.7 11.4 %collective-permute-start.1 = (bf16[2,128,128]{2,1,0:T(8,128)(2,1)S(1)}, bf16[2,128,128]{2,1,0:T(8,128)(2,1)S(1)}, u32[]{:S(2)}, u32[]{:S(2)}) collective-permute-start(bf16[2,128,128]{2,1,0:T(8,128)(2,1)S(1)} %get-tuple-element.107), channel_id=1, source_target_pairs={{240,0},{0,16},{16,32},{32,48},{48,64},{64,80},{80,96},{96,112},{1... | collective-permute-start | bytes 196616 | tf_op jit(solution)/shard_map/while/body/eval_jaxpr/ppermute | solution.py:10
  75.1 10.0 %collective-permute-start = (bf16[2,4,128,128]{3,2,1,0:T(8,128)(2,1)S(1)}, bf16[2,4,128,128]{3,2,1,0:T(8,128)(2,1)S(1)}, u32[]{:S(2)}, u32[]{:S(2)}) collective-permute-start(bf16[2,4,128,128]{3,2,1,0:T(8,128)(2,1)S(1)} %get-tuple-element.108), channel_id=1, source_target_pairs={{240,0},{0,16},{16,32},{32,48},{48,64},{64,80},{80,96},{96,112},{1... | collective-permute-start | bytes 786440 | tf_op jit(solution)/shard_map/while/body/eval_jaxpr/ppermute | solution.py:10
  75.1 10.0 %collective-permute-start.1 = (bf16[2,128,128]{2,1,0:T(8,128)(2,1)S(1)}, bf16[2,128,128]{2,1,0:T(8,128)(2,1)S(1)}, u32[]{:S(2)}, u32[]{:S(2)}) collective-permute-start(bf16[2,128,128]{2,1,0:T(8,128)(2,1)S(1)} %get-tuple-element.107), channel_id=1, source_target_pairs={{240,0},{0,16},{16,32},{32,48},{48,64},{64,80},{80,96},{96,112},{1... | collective-permute-start | bytes 196616 | tf_op jit(solution)/shard_map/while/body/eval_jaxpr/ppermute | solution.py:10
  96.1 9.2 %collective-permute-start = (bf16[2,4,128,128]{3,2,1,0:T(8,128)(2,1)S(1)}, bf16[2,4,128,128]{3,2,1,0:T(8,128)(2,1)S(1)}, u32[]{:S(2)}, u32[]{:S(2)}) collective-permute-start(bf16[2,4,128,128]{3,2,1,0:T(8,128)(2,1)S(1)} %get-tuple-element.108), channel_id=1, source_target_pairs={{240,0},{0,16},{16,32},{32,48},{48,64},{64,80},{80,96},{96,112},{1... | collective-permute-start | bytes 786440 | tf_op jit(solution)/shard_map/while/body/eval_jaxpr/ppermute | solution.py:10
  96.1 9.2 %collective-permute-start.1 = (bf16[2,128,128]{2,1,0:T(8,128)(2,1)S(1)}, bf16[2,128,128]{2,1,0:T(8,128)(2,1)S(1)}, u32[]{:S(2)}, u32[]{:S(2)}) collective-permute-start(bf16[2,128,128]{2,1,0:T(8,128)(2,1)S(1)} %get-tuple-element.107), channel_id=1, source_target_pairs={{240,0},{0,16},{16,32},{32,48},{48,64},{64,80},{80,96},{96,112},{1... | collective-permute-start | bytes 196616 | tf_op jit(solution)/shard_map/while/body/eval_jaxpr/ppermute | solution.py:10
  116.3 8.0 %collective-permute-start = (bf16[2,4,128,128]{3,2,1,0:T(8,128)(2,1)S(1)}, bf16[2,4,128,128]{3,2,1,0:T(8,128)(2,1)S(1)}, u32[]{:S(2)}, u32[]{:S(2)}) collective-permute-start(bf16[2,4,128,128]{3,2,1,0:T(8,128)(2,1)S(1)} %get-tuple-element.108), channel_id=1, source_target_pairs={{240,0},{0,16},{16,32},{32,48},{48,64},{64,80},{80,96},{96,112},{1... | collective-permute-start | bytes 786440 | tf_op jit(solution)/shard_map/while/body/eval_jaxpr/ppermute | solution.py:10
  116.3 8.0 %collective-permute-start.1 = (bf16[2,128,128]{2,1,0:T(8,128)(2,1)S(1)}, bf16[2,128,128]{2,1,0:T(8,128)(2,1)S(1)}, u32[]{:S(2)}, u32[]{:S(2)}) collective-permute-start(bf16[2,128,128]{2,1,0:T(8,128)(2,1)S(1)} %get-tuple-element.107), channel_id=1, source_target_pairs={{240,0},{0,16},{16,32},{32,48},{48,64},{64,80},{80,96},{96,112},{1... | collective-permute-start | bytes 196616 | tf_op jit(solution)/shard_map/while/body/eval_jaxpr/ppermute | solution.py:10
  135.4 8.0 %collective-permute-start = (bf16[2,4,128,128]{3,2,1,0:T(8,128)(2,1)S(1)}, bf16[2,4,128,128]{3,2,1,0:T(8,128)(2,1)S(1)}, u32[]{:S(2)}, u32[]{:S(2)}) collective-permute-start(bf16[2,4,128,128]{3,2,1,0:T(8,128)(2,1)S(1)} %get-tuple-element.108), channel_id=1, source_target_pairs={{240,0},{0,16},{16,32},{32,48},{48,64},{64,80},{80,96},{96,112},{1... | collective-permute-start | bytes 786440 | tf_op jit(solution)/shard_map/while/body/eval_jaxpr/ppermute | solution.py:10
  135.4 8.0 %collective-permute-start.1 = (bf16[2,128,128]{2,1,0:T(8,128)(2,1)S(1)}, bf16[2,128,128]{2,1,0:T(8,128)(2,1)S(1)}, u32[]{:S(2)}, u32[]{:S(2)}) collective-permute-start(bf16[2,128,128]{2,1,0:T(8,128)(2,1)S(1)} %get-tuple-element.107), channel_id=1, source_target_pairs={{240,0},{0,16},{16,32},{32,48},{48,64},{64,80},{80,96},{96,112},{1... | collective-permute-start | bytes 196616 | tf_op jit(solution)/shard_map/while/body/eval_jaxpr/ppermute | solution.py:10
  154.4 8.0 %collective-permute-start = (bf16[2,4,128,128]{3,2,1,0:T(8,128)(2,1)S(1)}, bf16[2,4,128,128]{3,2,1,0:T(8,128)(2,1)S(1)}, u32[]{:S(2)}, u32[]{:S(2)}) collective-permute-start(bf16[2,4,128,128]{3,2,1,0:T(8,128)(2,1)S(1)} %get-tuple-element.108), channel_id=1, source_target_pairs={{240,0},{0,16},{16,32},{32,48},{48,64},{64,80},{80,96},{96,112},{1... | collective-permute-start | bytes 786440 | tf_op jit(solution)/shard_map/while/body/eval_jaxpr/ppermute | solution.py:10
  154.4 8.0 %collective-permute-start.1 = (bf16[2,128,128]{2,1,0:T(8,128)(2,1)S(1)}, bf16[2,128,128]{2,1,0:T(8,128)(2,1)S(1)}, u32[]{:S(2)}, u32[]{:S(2)}) collective-permute-start(bf16[2,128,128]{2,1,0:T(8,128)(2,1)S(1)} %get-tuple-element.107), channel_id=1, source_target_pairs={{240,0},{0,16},{16,32},{32,48},{48,64},{64,80},{80,96},{96,112},{1... | collective-permute-start | bytes 196616 | tf_op jit(solution)/shard_map/while/body/eval_jaxpr/ppermute | solution.py:10
  173.5 8.0 %collective-permute-start = (bf16[2,4,128,128]{3,2,1,0:T(8,128)(2,1)S(1)}, bf16[2,4,128,128]{3,2,1,0:T(8,128)(2,1)S(1)}, u32[]{:S(2)}, u32[]{:S(2)}) collective-permute-start(bf16[2,4,128,128]{3,2,1,0:T(8,128)(2,1)S(1)} %get-tuple-element.108), channel_id=1, source_target_pairs={{240,0},{0,16},{16,32},{32,48},{48,64},{64,80},{80,96},{96,112},{1... | collective-permute-start | bytes 786440 | tf_op jit(solution)/shard_map/while/body/eval_jaxpr/ppermute | solution.py:10
  173.5 8.0 %collective-permute-start.1 = (bf16[2,128,128]{2,1,0:T(8,128)(2,1)S(1)}, bf16[2,128,128]{2,1,0:T(8,128)(2,1)S(1)}, u32[]{:S(2)}, u32[]{:S(2)}) collective-permute-start(bf16[2,128,128]{2,1,0:T(8,128)(2,1)S(1)} %get-tuple-element.107), channel_id=1, source_target_pairs={{240,0},{0,16},{16,32},{32,48},{48,64},{64,80},{80,96},{96,112},{1... | collective-permute-start | bytes 196616 | tf_op jit(solution)/shard_map/while/body/eval_jaxpr/ppermute | solution.py:10
  192.5 8.0 %collective-permute-start = (bf16[2,4,128,128]{3,2,1,0:T(8,128)(2,1)S(1)}, bf16[2,4,128,128]{3,2,1,0:T(8,128)(2,1)S(1)}, u32[]{:S(2)}, u32[]{:S(2)}) collective-permute-start(bf16[2,4,128,128]{3,2,1,0:T(8,128)(2,1)S(1)} %get-tuple-element.108), channel_id=1, source_target_pairs={{240,0},{0,16},{16,32},{32,48},{48,64},{64,80},{80,96},{96,112},{1... | collective-permute-start | bytes 786440 | tf_op jit(solution)/shard_map/while/body/eval_jaxpr/ppermute | solution.py:10
  192.5 8.0 %collective-permute-start.1 = (bf16[2,128,128]{2,1,0:T(8,128)(2,1)S(1)}, bf16[2,128,128]{2,1,0:T(8,128)(2,1)S(1)}, u32[]{:S(2)}, u32[]{:S(2)}) collective-permute-start(bf16[2,128,128]{2,1,0:T(8,128)(2,1)S(1)} %get-tuple-element.107), channel_id=1, source_target_pairs={{240,0},{0,16},{16,32},{32,48},{48,64},{64,80},{80,96},{96,112},{1... | collective-permute-start | bytes 196616 | tf_op jit(solution)/shard_map/while/body/eval_jaxpr/ppermute | solution.py:10
  211.6 8.0 %collective-permute-start = (bf16[2,4,128,128]{3,2,1,0:T(8,128)(2,1)S(1)}, bf16[2,4,128,128]{3,2,1,0:T(8,128)(2,1)S(1)}, u32[]{:S(2)}, u32[]{:S(2)}) collective-permute-start(bf16[2,4,128,128]{3,2,1,0:T(8,128)(2,1)S(1)} %get-tuple-element.108), channel_id=1, source_target_pairs={{240,0},{0,16},{16,32},{32,48},{48,64},{64,80},{80,96},{96,112},{1... | collective-permute-start | bytes 786440 | tf_op jit(solution)/shard_map/while/body/eval_jaxpr/ppermute | solution.py:10
  211.6 8.0 %collective-permute-start.1 = (bf16[2,128,128]{2,1,0:T(8,128)(2,1)S(1)}, bf16[2,128,128]{2,1,0:T(8,128)(2,1)S(1)}, u32[]{:S(2)}, u32[]{:S(2)}) collective-permute-start(bf16[2,128,128]{2,1,0:T(8,128)(2,1)S(1)} %get-tuple-element.107), channel_id=1, source_target_pairs={{240,0},{0,16},{16,32},{32,48},{48,64},{64,80},{80,96},{96,112},{1... | collective-permute-start | bytes 196616 | tf_op jit(solution)/shard_map/while/body/eval_jaxpr/ppermute | solution.py:10
  230.6 8.0 %collective-permute-start = (bf16[2,4,128,128]{3,2,1,0:T(8,128)(2,1)S(1)}, bf16[2,4,128,128]{3,2,1,0:T(8,128)(2,1)S(1)}, u32[]{:S(2)}, u32[]{:S(2)}) collective-permute-start(bf16[2,4,128,128]{3,2,1,0:T(8,128)(2,1)S(1)} %get-tuple-element.108), channel_id=1, source_target_pairs={{240,0},{0,16},{16,32},{32,48},{48,64},{64,80},{80,96},{96,112},{1... | collective-permute-start | bytes 786440 | tf_op jit(solution)/shard_map/while/body/eval_jaxpr/ppermute | solution.py:10
  230.6 8.0 %collective-permute-start.1 = (bf16[2,128,128]{2,1,0:T(8,128)(2,1)S(1)}, bf16[2,128,128]{2,1,0:T(8,128)(2,1)S(1)}, u32[]{:S(2)}, u32[]{:S(2)}) collective-permute-start(bf16[2,128,128]{2,1,0:T(8,128)(2,1)S(1)} %get-tuple-element.107), channel_id=1, source_target_pairs={{240,0},{0,16},{16,32},{32,48},{48,64},{64,80},{80,96},{96,112},{1... | collective-permute-start | bytes 196616 | tf_op jit(solution)/shard_map/while/body/eval_jaxpr/ppermute | solution.py:10
  249.7 8.0 %collective-permute-start = (bf16[2,4,128,128]{3,2,1,0:T(8,128)(2,1)S(1)}, bf16[2,4,128,128]{3,2,1,0:T(8,128)(2,1)S(1)}, u32[]{:S(2)}, u32[]{:S(2)}) collective-permute-start(bf16[2,4,128,128]{3,2,1,0:T(8,128)(2,1)S(1)} %get-tuple-element.108), channel_id=1, source_target_pairs={{240,0},{0,16},{16,32},{32,48},{48,64},{64,80},{80,96},{96,112},{1... | collective-permute-start | bytes 786440 | tf_op jit(solution)/shard_map/while/body/eval_jaxpr/ppermute | solution.py:10
  249.7 8.0 %collective-permute-start.1 = (bf16[2,128,128]{2,1,0:T(8,128)(2,1)S(1)}, bf16[2,128,128]{2,1,0:T(8,128)(2,1)S(1)}, u32[]{:S(2)}, u32[]{:S(2)}) collective-permute-start(bf16[2,128,128]{2,1,0:T(8,128)(2,1)S(1)} %get-tuple-element.107), channel_id=1, source_target_pairs={{240,0},{0,16},{16,32},{32,48},{48,64},{64,80},{80,96},{96,112},{1... | collective-permute-start | bytes 196616 | tf_op jit(solution)/shard_map/while/body/eval_jaxpr/ppermute | solution.py:10
  268.7 8.0 %collective-permute-start = (bf16[2,4,128,128]{3,2,1,0:T(8,128)(2,1)S(1)}, bf16[2,4,128,128]{3,2,1,0:T(8,128)(2,1)S(1)}, u32[]{:S(2)}, u32[]{:S(2)}) collective-permute-start(bf16[2,4,128,128]{3,2,1,0:T(8,128)(2,1)S(1)} %get-tuple-element.108), channel_id=1, source_target_pairs={{240,0},{0,16},{16,32},{32,48},{48,64},{64,80},{80,96},{96,112},{1... | collective-permute-start | bytes 786440 | tf_op jit(solution)/shard_map/while/body/eval_jaxpr/ppermute | solution.py:10
  268.7 8.0 %collective-permute-start.1 = (bf16[2,128,128]{2,1,0:T(8,128)(2,1)S(1)}, bf16[2,128,128]{2,1,0:T(8,128)(2,1)S(1)}, u32[]{:S(2)}, u32[]{:S(2)}) collective-permute-start(bf16[2,128,128]{2,1,0:T(8,128)(2,1)S(1)} %get-tuple-element.107), channel_id=1, source_target_pairs={{240,0},{0,16},{16,32},{32,48},{48,64},{64,80},{80,96},{96,112},{1... | collective-permute-start | bytes 196616 | tf_op jit(solution)/shard_map/while/body/eval_jaxpr/ppermute | solution.py:10
  287.8 8.0 %collective-permute-start = (bf16[2,4,128,128]{3,2,1,0:T(8,128)(2,1)S(1)}, bf16[2,4,128,128]{3,2,1,0:T(8,128)(2,1)S(1)}, u32[]{:S(2)}, u32[]{:S(2)}) collective-permute-start(bf16[2,4,128,128]{3,2,1,0:T(8,128)(2,1)S(1)} %get-tuple-element.108), channel_id=1, source_target_pairs={{240,0},{0,16},{16,32},{32,48},{48,64},{64,80},{80,96},{96,112},{1... | collective-permute-start | bytes 786440 | tf_op jit(solution)/shard_map/while/body/eval_jaxpr/ppermute | solution.py:10
  287.8 8.0 %collective-permute-start.1 = (bf16[2,128,128]{2,1,0:T(8,128)(2,1)S(1)}, bf16[2,128,128]{2,1,0:T(8,128)(2,1)S(1)}, u32[]{:S(2)}, u32[]{:S(2)}) collective-permute-start(bf16[2,128,128]{2,1,0:T(8,128)(2,1)S(1)} %get-tuple-element.107), channel_id=1, source_target_pairs={{240,0},{0,16},{16,32},{32,48},{48,64},{64,80},{80,96},{96,112},{1... | collective-permute-start | bytes 196616 | tf_op jit(solution)/shard_map/while/body/eval_jaxpr/ppermute | solution.py:10
  306.8 8.0 %collective-permute-start = (bf16[2,4,128,128]{3,2,1,0:T(8,128)(2,1)S(1)}, bf16[2,4,128,128]{3,2,1,0:T(8,128)(2,1)S(1)}, u32[]{:S(2)}, u32[]{:S(2)}) collective-permute-start(bf16[2,4,128,128]{3,2,1,0:T(8,128)(2,1)S(1)} %get-tuple-element.108), channel_id=1, source_target_pairs={{240,0},{0,16},{16,32},{32,48},{48,64},{64,80},{80,96},{96,112},{1... | collective-permute-start | bytes 786440 | tf_op jit(solution)/shard_map/while/body/eval_jaxpr/ppermute | solution.py:10
  306.8 8.0 %collective-permute-start.1 = (bf16[2,128,128]{2,1,0:T(8,128)(2,1)S(1)}, bf16[2,128,128]{2,1,0:T(8,128)(2,1)S(1)}, u32[]{:S(2)}, u32[]{:S(2)}) collective-permute-start(bf16[2,128,128]{2,1,0:T(8,128)(2,1)S(1)} %get-tuple-element.107), channel_id=1, source_target_pairs={{240,0},{0,16},{16,32},{32,48},{48,64},{64,80},{80,96},{96,112},{1... | collective-permute-start | bytes 196616 | tf_op jit(solution)/shard_map/while/body/eval_jaxpr/ppermute | solution.py:10
  325.9 8.0 %collective-permute-start = (bf16[2,4,128,128]{3,2,1,0:T(8,128)(2,1)S(1)}, bf16[2,4,128,128]{3,2,1,0:T(8,128)(2,1)S(1)}, u32[]{:S(2)}, u32[]{:S(2)}) collective-permute-start(bf16[2,4,128,128]{3,2,1,0:T(8,128)(2,1)S(1)} %get-tuple-element.108), channel_id=1, source_target_pairs={{240,0},{0,16},{16,32},{32,48},{48,64},{64,80},{80,96},{96,112},{1... | collective-permute-start | bytes 786440 | tf_op jit(solution)/shard_map/while/body/eval_jaxpr/ppermute | solution.py:10
  325.9 8.0 %collective-permute-start.1 = (bf16[2,128,128]{2,1,0:T(8,128)(2,1)S(1)}, bf16[2,128,128]{2,1,0:T(8,128)(2,1)S(1)}, u32[]{:S(2)}, u32[]{:S(2)}) collective-permute-start(bf16[2,128,128]{2,1,0:T(8,128)(2,1)S(1)} %get-tuple-element.107), channel_id=1, source_target_pairs={{240,0},{0,16},{16,32},{32,48},{48,64},{64,80},{80,96},{96,112},{1... | collective-permute-start | bytes 196616 | tf_op jit(solution)/shard_map/while/body/eval_jaxpr/ppermute | solution.py:10
  344.9 25.0 %copy-start.1 = (s32[16,1]{0,1:T(1,128)S(1)}, s32[16,1]{0,1:T(1,128)}, u32[]{:S(2)}) copy-start(s32[16,1]{0,1:T(1,128)} %param.10) | copy-start | bytes 196
  347.7 39.5 %all-to-all-start.2 = ((bf16[16,2,128,128]{3,2,1,0:T(8,128)(2,1)}), bf16[16,2,128,128]{3,2,1,0:T(8,128)(2,1)S(1)}, u32[]{:S(2)}, u32[]{:S(2)}) async-start(bf16[16,2,128,128]{3,2,1,0:T(8,128)(2,1)} %bitcast.21), calls=%async_computation.2 | async-start | bytes 2097152 | tf_op jit(solution)/shard_map/all_to_all | solution.py:80
where the time goes:
time: 390 us; the launch traced here: 389 us
  waiting for transfers between devices  159 us (41%)
  matrix products  121 us (31%)
  local copies, waits for them, and re-layouts  60.1 us (15%)
  starting transfers between devices  38.8 us (10%)
  other arithmetic  8.89 us (2%)
    ppermute x30, waiting for transfers between devices, from_behind(): return lax.ppermute(block, axis, route)  125 us
    dot_general x32, matrix products, apply_terms(): jnp.einsum('kac,kdc->kad', mixed_left, chosen, preferred_element_type=jnp...  121 us
    gather x32, local copies, waits for them, and re-layouts, apply_terms(): chosen = jnp.take(right_now[index_term], slot_right, axis=0)  53.1 us
    all_to_all x1, starting transfers between devices, local(): lax.all_to_all(out_slots, 'sector', split_axis=0, concat_axis=0, tiled=True)  22.3 us
    all_to_all x1, waiting for transfers between devices, local(): lax.all_to_all(out_slots, 'sector', split_axis=0, concat_axis=0, tiled=True)  17.2 us
    all_to_all x1, waiting for transfers between devices, local(): lax.all_to_all(sent_wave.reshape(n_sec, capacity, order, order), 'sector'...  12.8 us
    all_to_all x1, starting transfers between devices, local(): lax.all_to_all(sent_right.reshape(n_sec, capacity), 'sector', split_axis=...  8.44 us
  transfers between devices with their start and end apart: 33, of which 18 were waited for; matrix products, arithmetic and copies ran while one was open for 2% of the time, Pallas kernels for 0%

commit v1 on v0

v1 whole, which is shorter than its diff:
```python
import functools

import jax
import jax.numpy as jnp
from jax import lax
from jax.experimental import pallas as pl
from jax.experimental.pallas import tpu as pltpu
from jax.sharding import PartitionSpec as P

CHUNKS = 1
UNROLL = 8
MESH = pl.DeviceIdType.MESH
SEQUENCE = ("B1", "B2", "A1", "X1", "B3", "X2", "B4", "A2", "X3", "X4", "A3", "A4")


def kernel(
    x_in, i_in, l_in, r_in, o_ref, *scratch
):
    chunks = CHUNKS
    W = scratch[:chunks]
    (x_all, i_all, i_smem, part, acc, got_core, got_y,
     send_sem, swap_sem, h_sem, ax_sem, az_sem, bz_sem, bx_sem, x_sem, i_sem, red_sem, loc_sem) = scratch[chunks:]
    held, order = x_in.shape[0], x_in.shape[1]
    rows = order // chunks
    term, sector = lax.axis_index("term"), lax.axis_index("sector")
    p, z = term // 8, lax.rem(term, 8)
    h, x, c = sector // 8, lax.rem(sector // 2, 4), lax.rem(sector, 2)
    turn = 1 - 2 * c
    core = (term, sector + turn)
    across = (lax.rem(term + 8, 16), sector)
    twin = (term, lax.rem(sector + 8, 16))

    def z_at(k):
        return lax.rem(z + 16 + k * turn, 8)

    def x_at(k):
        return lax.rem(x + 8 + k * turn, 4)

    def z_dev(k):
        return (p * 8 + z_at(k), sector)

    def x_dev(k):
        return (term, h * 8 + x_at(k) * 2 + c)

    barrier = pltpu.get_barrier_semaphore()
    peers = (core, across, twin, z_dev(1), z_dev(-1), x_dev(1), x_dev(-1))
    for peer in peers:
        pl.semaphore_signal(barrier, inc=1, device_id=peer, device_id_type=MESH)
    pl.semaphore_wait(barrier, len(peers))

    pending = []

    def copy_of(src, dst, recv, device, number=0):
        return pltpu.make_async_remote_copy(
            src_ref=src, dst_ref=dst, send_sem=send_sem.at[number], recv_sem=recv,
            device_id=device, device_id_type=MESH,
        )

    def send(src, dst, recv, device):
        made = copy_of(src, dst, recv, device, len(pending))
        made.start()
        pending.append(made)

    def arrived(dst, recv):
        copy_of(dst, dst, recv, core).wait_recv()

    def width(q):
        return 2 + (chunks if q == 0 else 0)

    def b_at(q, xx):
        return 8 + xx * width(q)

    def item(q, e):
        return z_at(-e) if e <= 4 else z_at(e - 4)

    def a_pair(q, e, xx):
        return W[q].at[item(q, e), pl.ds(2 * xx, 2)]

    def a_row(q, e):
        return W[q].at[item(q, e), pl.ds(0, 8)]

    def b_item(q, e, xx):
        return W[q].at[item(q, e), pl.ds(b_at(q, xx), width(q))]

    local = []
    for q in range(chunks):
        mine = jnp.where(c == 0, 2 * x + h, b_at(q, x) + h)
        send(l_in.at[1 - c, q], W[q].at[z, mine], swap_sem.at[q], core)
        local.append(pltpu.make_async_copy(l_in.at[c, q], W[q].at[z, mine], loc_sem.at[q]))
        local[-1].start()
    right_own = pltpu.make_async_copy(
        r_in.at[c, x], W[0].at[z, pl.ds(b_at(0, x) + 2, chunks)], loc_sem.at[chunks])
    right_own.start()
    for q in range(chunks):
        other = jnp.where(c == 0, b_at(q, x) + h, 2 * x + h)
        local[q].wait()
        arrived(W[q].at[z, other], swap_sem.at[q])
        for kind, slot in ((0, 2 * x + h), (1, b_at(q, x) + h)):
            send(W[q].at[z, slot], W[q].at[z, slot], h_sem.at[q, kind], twin)
    right_own.wait()
    send(i_in, i_all.at[1], i_sem.at[1], core)
    send(i_in, i_all.at[2], i_sem.at[2], across)
    send(x_in, x_all.at[1], x_sem.at[1], core)
    send(x_in, x_all.at[2], x_sem.at[2], across)
    keep = pltpu.make_async_copy(i_in, i_all.at[0], loc_sem.at[chunks + 1])
    keep.start()
    keep_x = pltpu.make_async_copy(x_in, x_all.at[0], loc_sem.at[chunks + 2])
    keep_x.start()

    def x_sends(q, e):
        mine = b_item(q, e, x)
        send(mine, mine, bx_sem.at[q, e, 0], x_dev(1))
        send(mine, mine, bx_sem.at[q, e, 1], x_dev(-1))

    def x_forward(q, e):
        passed = b_item(q, e, x_at(-1))
        arrived(passed, bx_sem.at[q, e, 0])
        send(passed, passed, bx_sem.at[q, e, 2], x_dev(1))

    def opening(q):
        for kind, slot in ((0, 2 * x + 1 - h), (1, b_at(q, x) + 1 - h)):
            arrived(W[q].at[z, slot], h_sem.at[q, kind])
        mine = b_item(q, 0, x)
        send(mine, mine, bz_sem.at[q, 1], z_dev(1))
        send(mine, mine, bz_sem.at[q, 5], z_dev(-1))
        pair = a_pair(q, 0, x)
        send(pair, pair, ax_sem.at[q, 0], x_dev(1))
        send(pair, pair, ax_sem.at[q, 1], x_dev(-1))
        x_sends(q, 0)

    def row_ready(q):
        passed = a_pair(q, 0, x_at(-1))
        arrived(passed, ax_sem.at[q, 0])
        send(passed, passed, ax_sem.at[q, 2], x_dev(1))
        arrived(a_pair(q, 0, x_at(1)), ax_sem.at[q, 1])
        arrived(a_pair(q, 0, x_at(2)), ax_sem.at[q, 2])
        row = a_row(q, 0)
        send(row, row, az_sem.at[q, 1], z_dev(1))
        send(row, row, az_sem.at[q, 5], z_dev(-1))

    def tick(q, what, d):
        for e, last, way in ((d, 4, 1), (4 + d, 7, -1)):
            if e > last:
                continue
            if what == "A":
                row = a_row(q, e)
                arrived(row, az_sem.at[q, e])
                if e < last:
                    send(row, row, az_sem.at[q, e + 1], z_dev(way))
            if what == "B":
                mine = b_item(q, e, x)
                arrived(mine, bz_sem.at[q, e])
                if e < last:
                    send(mine, mine, bz_sem.at[q, e + 1], z_dev(way))
                x_sends(q, e)
            if what == "X":
                x_forward(q, e)

    def closing(q):
        for e in range(8):
            arrived(b_item(q, e, x_at(1)), bx_sem.at[q, e, 1])
            arrived(b_item(q, e, x_at(2)), bx_sem.at[q, e, 2])

    def others():
        arrived(i_all.at[1], i_sem.at[1])
        arrived(i_all.at[2], i_sem.at[2])
        send(i_all.at[2], i_all.at[3], i_sem.at[3], core)
        arrived(x_all.at[2], x_sem.at[2])
        send(x_all.at[2], x_all.at[3], x_sem.at[3], core)
        arrived(x_all.at[1], x_sem.at[1])
        keep.wait()
        keep_x.wait()
        arrived(i_all.at[3], i_sem.at[3])
        table = pltpu.make_async_copy(i_all, i_smem, loc_sem.at[chunks + 3])
        table.start()
        arrived(x_all.at[3], x_sem.at[3])
        table.wait()

    def products(q, group, store):
        def some(i, carry):
            for u in range(UNROLL):
                k = i * UNROLL + u
                left, right = i_smem[group, 0, k], i_smem[group, 0, held + k]
                spot, half, odd = (left >> 1) & 3, left >> 3, left & 1
                slot = jnp.where(odd == 0, 2 * spot + half, b_at(q, spot) + half)
                tall = jnp.concatenate([W[q][e, slot] for e in range(8)], axis=0)
                mixed = jnp.dot(
                    tall, x_all[group, k], preferred_element_type=jnp.float32
                ).astype(jnp.bfloat16)
                wide = jnp.concatenate(
                    [mixed[e * rows:(e + 1) * rows] for e in range(8)], axis=1)
                at = b_at(0, right) + 2
                chosen = jnp.concatenate(
                    [jnp.concatenate([W[0][e, at + i] for i in range(chunks)], axis=0)
                     for e in range(8)], axis=1)
                store(k, lax.dot_general(
                    wide, chosen, (((1,), (1,)), ((), ())),
                    preferred_element_type=jnp.float32))
            return carry
        lax.fori_loop(0, held // UNROLL, some, 0)

    def put(ref):
        def store(k, value):
            ref[k] = value.astype(ref.dtype)
        return store

    def reduce_steps(q):
        def first():
            products(q, 3, put(part.at[q, 0]))
            send(part.at[q, 0], got_core.at[q, 0], red_sem.at[q, 0], core)

        def second():
            products(q, 2, put(acc))
            arrived(got_core.at[q, 0], red_sem.at[q, 0])

            def join(k, carry):
                part[q, 1, k] = (acc[k] + got_core[q, 0, k].astype(jnp.float32)).astype(jnp.bfloat16)
                return carry
            lax.fori_loop(0, held, join, 0)
            send(part.at[q, 1], got_y.at[q], red_sem.at[q, 1], across)

        def third():
            products(q, 1, put(part.at[q, 2]))
            send(part.at[q, 2], got_core.at[q, 1], red_sem.at[q, 2], core)

        def fourth():
            products(q, 0, put(acc))
            arrived(got_core.at[q, 1], red_sem.at[q, 2])
            arrived(got_y.at[q], red_sem.at[q, 1])

            def join(k, carry):
                total = acc[k] + got_core[q, 1, k].astype(jnp.float32) + got_y[q, k].astype(jnp.float32)
                o_ref[k, pl.ds(q * rows, rows)] = total.astype(jnp.bfloat16)
                return carry
            lax.fori_loop(0, held, join, 0)
        return [first, second, third, fourth]

    for q in range(chunks):
        opening(q)
    for q in range(chunks):
        x_forward(q, 0)
        row_ready(q)
    waiting = []
    for q in range(chunks):
        steps = [functools.partial(tick, q, name[0], int(name[1])) for name in SEQUENCE]
        for number, step in enumerate(steps):
            step()
            if waiting and number % 3 == 2:
                waiting.pop(0)()
        closing(q)
        if q == 0:
            others()
        for step in waiting:
            step()
        waiting = reduce_steps(q)
    for step in waiting:
        step()
    for made in pending:
        made.wait_send()


def local(wavefunction, left_sector, right_sector, left_blocks, right_blocks):
    held, order = wavefunction.shape[:2]
    rows = order // CHUNKS
    index = jnp.concatenate([left_sector[:, 0], right_sector])
    index = jnp.pad(index[None], ((0, 7), (0, 128 - 2 * held)))
    left = left_blocks.reshape(2, CHUNKS, rows, order)
    right = right_blocks.reshape(2, 4, CHUNKS, rows, order)
    bf16 = jnp.bfloat16
    dma = pltpu.SemaphoreType.DMA
    scratch = [
        pltpu.VMEM((8, 8 + 4 * (2 + (CHUNKS if q == 0 else 0)), rows, order), bf16)
        for q in range(CHUNKS)
    ]
    scratch += [
        pltpu.VMEM((4, held, order, order), bf16),
        pltpu.VMEM((4, 8, 128), jnp.int32),
        pltpu.SMEM((4, 8, 128), jnp.int32),
        pltpu.VMEM((CHUNKS, 3, held, rows, order), bf16),
        pltpu.VMEM((held, rows, order), jnp.float32),
        pltpu.VMEM((CHUNKS, 2, held, rows, order), bf16),
        pltpu.VMEM((CHUNKS, held, rows, order), bf16),
        dma((6 + 50 * CHUNKS,)),
        dma((CHUNKS,)),
        dma((CHUNKS, 2)),
        dma((CHUNKS, 3)),
        dma((CHUNKS, 8)),
        dma((CHUNKS, 8)),
        dma((CHUNKS, 8, 3)),
        dma((4,)),
        dma((4,)),
        dma((CHUNKS, 3)),
        dma((CHUNKS + 4,)),
    ]
    vmem = pl.BlockSpec(memory_space=pltpu.VMEM)
    return pl.pallas_call(
        kernel,
        out_shape=jax.ShapeDtypeStruct(wavefunction.shape, wavefunction.dtype),
        in_specs=[vmem] * 4,
        out_specs=vmem,
        scratch_shapes=scratch,
        compiler_params=pltpu.CompilerParams(
            collective_id=0, has_side_effects=True, vmem_limit_bytes=48 * 1024 * 1024),
        name="terms",
    )(wavefunction, index, left, right)


def solution(mesh):
    placed = (
        P(("term", "sector"), None, None),
        P(("term", "sector"), None),
        P(("term", "sector")),
        P("term", "sector", None, None),
        P("term", None, None, None),
    )
    return jax.shard_map(
        local,
        mesh=mesh,
        in_specs=placed,
        out_specs=P(("term", "sector"), None, None),
        check_vma=False,
    )
```

time: 390 us -> 80.9 us (0.21)
  waiting for transfers between devices: 159 us -> 0 us
  matrix products: 121 us -> 0 us
  Pallas kernels: 0 us -> 76.3 us
  local copies, waits for them, and re-layouts: 60.1 us -> 4.3 us
  starting transfers between devices: 38.8 us -> 0 us
  other arithmetic: 8.89 us -> 0.07 us
    ppermute x30 -> x0, waiting for transfers between devices: 125 us -> none  [from_behind(): return lax.ppermute(block, axis, route)]
    dot_general x32 -> x0, matrix products: 121 us -> none  [apply_terms(): jnp.einsum('kac,kdc->kad', mixed_left, chosen, preferred_element_type=jnp...]
    pallas_call x0 -> x1, Pallas kernels: none -> 76.3 us  [local(): pl.pallas_call(kernel, out_shape=jax.ShapeDtypeStruct(wavefunction.shape,...]
    gather x37 -> x0, local copies, waits for them, and re-layouts: 56.6 us -> none  [the longest x32 53.1 us: apply_terms(): chosen = jnp.take(right_now[index_term], slot_right, axis=0)]
    all_to_all x3 -> x0, starting transfers between devices: 35.4 us -> none  [the longest x1 22.3 us: local(): lax.all_to_all(out_slots, 'sector', split_axis=0, concat_axis=0, tiled=True)]
    all_to_all x3 -> x0, waiting for transfers between devices: 34.1 us -> none  [the longest x1 17.2 us: local(): lax.all_to_all(out_slots, 'sector', split_axis=0, concat_axis=0, tiled=True)]
  transfers between devices with their start and end apart: 33 -> 0, of which waited for: 18 -> 0; matrix products, arithmetic and copies ran while one was open for 2% -> 0% of each run, Pallas kernels for 0% -> 0%
where the time goes in v1:
time: 80.9 us; the launch traced here: 80.7 us
  Pallas kernels  76.3 us (94%)
  local copies, waits for them, and re-layouts  4.3 us (5%)
    pallas_call x1, Pallas kernels, local(): pl.pallas_call(kernel, out_shape=jax.ShapeDtypeStruct(wavefunction.shape,...  76.3 us
    unnamed x11, local copies, waits for them, and re-layouts  4.29 us

profile of v1, /device:TPU:1, one launch (start us, length us, event | category | flops | bytes accessed | tf_op | source)
XLA Modules:
  0.0 80.7 jit_solution(17912126457639195963)
XLA Ops:
  0.0 0.0 copy-start.3
  0.0 0.0 copy-start.4
  0.0 0.7 copy-done.3
  0.7 0.0 copy-done.4
  0.7 0.1 add_bitcast_fusion
  0.8 0.0 copy-start
  0.8 1.0 %copy-done = bf16[16,128,128]{2,1,0:T(8,128)(2,1)S(1)} copy-done((bf16[16,128,128]{2,1,0:T(8,128)(2,1)S(1)}, bf16[16,128,128]{2,1,0:T(8,128)(2,1)}, u32[]{:S(2)}) %copy-start) | copy-done | bytes 524312
  1.8 0.0 copy-start.1
  1.8 0.9 %copy-done.1 = bf16[2,4,128,128]{3,2,1,0:T(8,128)(2,1)S(1)} copy-done((bf16[2,4,128,128]{3,2,1,0:T(8,128)(2,1)S(1)}, bf16[2,4,128,128]{3,2,1,0:T(8,128)(2,1)}, u32[]{:S(2)}) %copy-start.1) | copy-done | bytes 262168
  2.7 0.0 copy-start.2
  2.8 0.8 %copy-done.2 = bf16[2,1,128,128]{3,2,1,0:T(8,128)(2,1)S(1)} copy-done((bf16[2,1,128,128]{3,2,1,0:T(8,128)(2,1)S(1)}, bf16[2,1,128,128]{3,2,1,0:T(8,128)(2,1)}, u32[]{:S(2)}) %copy-start.2) | copy-done | bytes 65560
  3.6 76.3 %terms.1 = bf16[16,128,128]{2,1,0:T(8,128)(2,1)S(1)} custom-call(bf16[16,128,128]{2,1,0:T(8,128)(2,1)S(1)} %copy-done, s32[8,128]{1,0:T(8,128)S(1)} %pad.4.i_in, bf16[2,1,128,128]{3,2,1,0:T(8,128)(2,1)S(1)} %copy-done.2, bf16[2,4,1,128,128]{4,3,2,1,0:T(8,128)(2,1)S(1)} %bitcast.4), custom_call_target="tpu_custom_call" | custom-call | tf_op jit(solution)/shard_map/terms/pallas_call | solution.py:296
  79.9 0.8 copy.7
  (1 shorter events, 0.0 us)
Async XLA Ops:
  0.0 0.7 copy-start.3
  0.0 0.7 copy-start.4
  0.8 1.0 %copy-start = (bf16[16,128,128]{2,1,0:T(8,128)(2,1)S(1)}, bf16[16,128,128]{2,1,0:T(8,128)(2,1)}, u32[]{:S(2)}) copy-start(bf16[16,128,128]{2,1,0:T(8,128)(2,1)} %x_in.1) | copy-start | bytes 1572868
  1.8 0.9 %copy-start.1 = (bf16[2,4,128,128]{3,2,1,0:T(8,128)(2,1)S(1)}, bf16[2,4,128,128]{3,2,1,0:T(8,128)(2,1)}, u32[]{:S(2)}) copy-start(bf16[2,4,128,128]{3,2,1,0:T(8,128)(2,1)} %param.9) | copy-start | bytes 786436
  2.7 0.8 %copy-start.2 = (bf16[2,1,128,128]{3,2,1,0:T(8,128)(2,1)S(1)}, bf16[2,1,128,128]{3,2,1,0:T(8,128)(2,1)}, u32[]{:S(2)}) copy-start(bf16[2,1,128,128]{3,2,1,0:T(8,128)(2,1)} %l_in.1) | copy-start | bytes 196612

commit v2 on v0

v2 whole, which is shorter than its diff:
```python
import functools

import jax
import jax.numpy as jnp
from jax import lax
from jax.experimental import pallas as pl
from jax.experimental.pallas import tpu as pltpu
from jax.sharding import PartitionSpec as P

CHUNKS = 2
PIECE = 8
MESH = pl.DeviceIdType.MESH
ORDER = (
    "0R", "1R", "0r", "0B1", "0X0", "0A1", "1r", "0B2", "0X1", "0A2", "0B3", "0X2", "0A3",
    "0B4", "0X3", "0A4", "1B1", "1X0", "1A1", "0X4", "1B2", "1X1", "1A2", "0C", "O", "0P0",
    "0P1", "1B3", "1X2", "1A3", "0P2", "0P3", "1B4", "1X3", "1A4", "0P4", "0P5", "1X4", "0P6",
    "0P7", "1C", "1P0", "1P1", "1P2", "1P3", "1P4", "1P5", "1P6", "1P7",
)


def kernel(x_in, i_in, l_in, r_in, o_ref, *scratch):
    chunks = CHUNKS
    W = scratch[:chunks]
    (x_all, i_all, i_smem, r_own, part, acc, got_core, got_y,
     send_sem, head_sem, a_sem, b_sem, az_sem, bz_sem, bx_sem, x_sem, i_sem, red_sem,
     loc_sem) = scratch[chunks:]
    held, order = x_in.shape[0], x_in.shape[1]
    rows = order // chunks
    term, sector = lax.axis_index("term"), lax.axis_index("sector")
    p, z = term // 8, lax.rem(term, 8)
    h, x, c = sector // 8, lax.rem(sector // 2, 4), lax.rem(sector, 2)
    turn = 1 - 2 * c
    core = (term, sector + turn)
    across = (lax.rem(term + 8, 16), sector)

    def z_at(k):
        return lax.rem(z + 16 + k * turn, 8)

    def x_at(k):
        return lax.rem(x + 8 + k * turn, 4)

    def z_dev(k):
        return (p * 8 + z_at(k), sector)

    def x_dev(k):
        return (term, h * 8 + x_at(k) * 2 + c)

    def plane(dh, dx, core_index):
        return (term, lax.rem(h + dh, 2) * 8 + lax.rem(x + dx, 4) * 2 + core_index)

    def width(q):
        return 2 + (chunks if q == 0 else 0)

    def b_at(q, xx):
        return 8 + xx * width(q)

    def item(e):
        return z_at(-e) if e <= 4 else z_at(e - 4)

    def a_half(q, e, half):
        return W[q].at[item(e), pl.ds(4 * half, 4)]

    def b_item(q, e, xx):
        return W[q].at[item(e), pl.ds(b_at(q, xx), width(q))]

    right_own = pltpu.make_async_copy(r_in.at[c, x], r_own, loc_sem.at[0])
    right_own.start()
    keep = pltpu.make_async_copy(i_in, i_all.at[0], loc_sem.at[1])
    keep.start()
    keep_x = pltpu.make_async_copy(x_in, x_all.at[0], loc_sem.at[2])
    keep_x.start()

    barrier = pltpu.get_barrier_semaphore()
    peers = [across, z_dev(1), z_dev(-1), core]
    for dh in range(2):
        for dx in range(4):
            if dh or dx:
                peers += [plane(dh, dx, 0), plane(dh, dx, 1)]
    for peer in peers:
        pl.semaphore_signal(barrier, inc=1, device_id=peer, device_id_type=MESH)

    right_own.wait()
    turned = r_own[...].T
    for i in range(chunks):
        W[0][z, b_at(0, x) + 2 + i] = turned[i * rows:(i + 1) * rows]

    pl.semaphore_wait(barrier, len(peers))

    pending, head0, head1 = [], [], []

    def send(src, dst, recv, device, kept=None):
        kept, sems = (pending, send_sem) if kept is None else (kept, head_sem)
        made = pltpu.make_async_remote_copy(
            src_ref=src, dst_ref=dst, send_sem=sems.at[len(kept)], recv_sem=recv,
            device_id=device, device_id_type=MESH)
        made.start()
        kept.append(made)

    def arrived(dst, recv):
        pltpu.make_async_remote_copy(
            src_ref=dst, dst_ref=dst, send_sem=send_sem.at[0], recv_sem=recv,
            device_id=core, device_id_type=MESH).wait_recv()

    def own_copy(q):
        slot = jnp.where(c == 0, 2 * x + h, b_at(q, x) + h)
        return pltpu.make_async_copy(l_in.at[c, q], W[q].at[z, slot], loc_sem.at[3 + q])

    for q in range(chunks):
        own_copy(q).start()

        @pl.when(c == 1)
        def _():
            slot = b_at(q, x) + h
            send(l_in.at[0, q], W[q].at[z, slot], b_sem.at[q, 0], core, head1)
            for j in range(2):
                send(l_in.at[j, q], W[q].at[z, slot], b_sem.at[q, 1], plane(1, 0, j), head1)

        @pl.when(c == 0)
        def _():
            slot = 2 * x + h
            for dh, dx in ((1, 2), (0, 2), (1, 1), (1, 3), (1, 0), (0, 1), (0, 3)):
                for j in range(2):
                    send(l_in.at[j, q], W[q].at[z, slot], a_sem.at[q, dh * 4 + dx],
                         plane(dh, dx, j), head0)
            send(l_in.at[1, q], W[q].at[z, slot], a_sem.at[q, 0], core, head0)

    def x_sends(q, e):
        mine = b_item(q, e, x)
        send(mine, mine, bx_sem.at[q, e, 0], x_dev(1))
        send(mine, mine, bx_sem.at[q, e, 1], x_dev(-1))

    def column_ready(q):
        @pl.when(c == 0)
        def _():
            arrived(W[q].at[z, b_at(q, x) + h], b_sem.at[q, 0])

        @pl.when(c == 1)
        def _():
            own_copy(q).wait()
        arrived(W[q].at[z, b_at(q, x) + 1 - h], b_sem.at[q, 1])
        mine = b_item(q, 0, x)
        send(mine, mine, bz_sem.at[q, 1], z_dev(1))
        send(mine, mine, bz_sem.at[q, 5], z_dev(-1))
        x_sends(q, 0)

    def row_ready(q):
        @pl.when(c == 0)
        def _():
            own_copy(q).wait()

        @pl.when(c == 1)
        def _():
            arrived(W[q].at[z, 2 * x + h], a_sem.at[q, 0])
        for dh in range(2):
            for dx in range(4):
                if dh or dx:
                    slot = 2 * lax.rem(x + 4 - dx, 4) + lax.rem(h + dh, 2)
                    arrived(W[q].at[z, slot], a_sem.at[q, dh * 4 + dx])
        for half in range(2):
            row = a_half(q, 0, half)
            send(row, row, az_sem.at[q, 1, half], z_dev(1))
            send(row, row, az_sem.at[q, 5, half], z_dev(-1))

    def ways(d):
        return [w for w in ((d, 4, 1), (4 + d, 7, -1)) if w[0] <= w[1]]

    def tick_a(q, d):
        for half in range(2):
            for e, last, way in ways(d):
                row = a_half(q, e, half)
                arrived(row, az_sem.at[q, e, half])
                if e < last:
                    send(row, row, az_sem.at[q, e + 1, half], z_dev(way))

    def tick_b(q, d):
        for e, last, way in ways(d):
            mine = b_item(q, e, x)
            arrived(mine, bz_sem.at[q, e])
            if e < last:
                send(mine, mine, bz_sem.at[q, e + 1], z_dev(way))
            x_sends(q, e)

    def tick_x(q, d):
        for e in ((0,) if d == 0 else [w[0] for w in ways(d)]):
            passed = b_item(q, e, x_at(-1))
            arrived(passed, bx_sem.at[q, e, 0])
            send(passed, passed, bx_sem.at[q, e, 2], x_dev(1))

    def closing(q):
        for e in range(8):
            arrived(b_item(q, e, x_at(1)), bx_sem.at[q, e, 1])
            arrived(b_item(q, e, x_at(2)), bx_sem.at[q, e, 2])

    def exchange():
        send(i_in, i_all.at[1], i_sem.at[1], core)
        send(i_in, i_all.at[2], i_sem.at[2], across)
        send(x_in, x_all.at[1], x_sem.at[1], core)
        send(x_in, x_all.at[2], x_sem.at[2], across)

    def others():
        arrived(i_all.at[1], i_sem.at[1])
        arrived(i_all.at[2], i_sem.at[2])
        send(i_all.at[2], i_all.at[3], i_sem.at[3], core)
        arrived(x_all.at[2], x_sem.at[2])
        send(x_all.at[2], x_all.at[3], x_sem.at[3], core)
        arrived(x_all.at[1], x_sem.at[1])
        keep.wait()
        keep_x.wait()
        arrived(i_all.at[3], i_sem.at[3])
        table = pltpu.make_async_copy(i_all, i_smem, loc_sem.at[3 + chunks])
        table.start()
        arrived(x_all.at[3], x_sem.at[3])
        table.wait()

    def products(q, group, first, store):
        for u in range(PIECE):
            k = first + u
            left, right = i_smem[group, 0, k], i_smem[group, 0, held + k]
            spot, half, odd = (left >> 1) & 3, left >> 3, left & 1
            slot = jnp.where(odd == 0, 2 * spot + half, b_at(q, spot) + half)
            tall = jnp.concatenate([W[q][e, slot] for e in range(8)], axis=0)
            mixed = jnp.dot(
                tall, x_all[group, k], preferred_element_type=jnp.float32
            ).astype(jnp.bfloat16)
            wide = jnp.concatenate([mixed[e * rows:(e + 1) * rows] for e in range(8)], axis=1)
            at = b_at(0, right) + 2
            chosen = jnp.concatenate(
                [W[0][e, at + i] for e in range(8) for i in range(chunks)], axis=0)
            store(k, jnp.dot(wide, chosen, preferred_element_type=jnp.float32))

    def piece(q, number):
        stage, first = number // 2, (number % 2) * PIECE
        span = pl.ds(first, PIECE)

        def to_part(k, value):
            part[q, stage, k] = value.astype(jnp.bfloat16)

        def to_acc(k, value):
            acc[k] = value
        if stage == 0:
            products(q, 3, first, to_part)
            send(part.at[q, 0, span], got_core.at[q, 0, span], red_sem.at[q, 0, number % 2], core)
        if stage == 1:
            products(q, 2, first, to_acc)
            arrived(got_core.at[q, 0, span], red_sem.at[q, 0, number % 2])
            part[q, 1, span] = (
                acc[span] + got_core[q, 0, span].astype(jnp.float32)).astype(jnp.bfloat16)
            send(part.at[q, 1, span], got_y.at[q, span], red_sem.at[q, 1, number % 2], across)
        if stage == 2:
            products(q, 1, first, to_part)
            send(part.at[q, 2, span], got_core.at[q, 1, span], red_sem.at[q, 2, number % 2], core)
        if stage == 3:
            products(q, 0, first, to_acc)
            arrived(got_core.at[q, 1, span], red_sem.at[q, 2, number % 2])
            arrived(got_y.at[q, span], red_sem.at[q, 1, number % 2])
            total = (acc[span] + got_core[q, 1, span].astype(jnp.float32)
                     + got_y[q, span].astype(jnp.float32))
            o_ref[span, pl.ds(q * rows, rows)] = total.astype(jnp.bfloat16)

    for name in ORDER:
        if name == "O":
            others()
            continue
        q, what, d = int(name[0]), name[1], int(name[2:] or 0)
        if what == "R":
            column_ready(q)
        if what == "r":
            row_ready(q)
            if q == 0:
                exchange()
        if what == "A":
            tick_a(q, d)
        if what == "B":
            tick_b(q, d)
        if what == "X":
            tick_x(q, d)
        if what == "C":
            closing(q)
        if what == "P":
            piece(q, d)

    for made in pending:
        made.wait_send()
    for kept, index in ((head0, 0), (head1, 1)):
        @pl.when(c == index)
        def _():
            for number in range(len(kept)):
                pltpu.make_async_remote_copy(
                    src_ref=l_in.at[0, 0], dst_ref=W[0].at[0, 0], send_sem=head_sem.at[number],
                    recv_sem=a_sem.at[0, 0], device_id=core, device_id_type=MESH).wait_send()


def local(wavefunction, left_sector, right_sector, left_blocks, right_blocks):
    held, order = wavefunction.shape[:2]
    rows = order // CHUNKS
    index = jnp.concatenate([left_sector[:, 0], right_sector])
    index = jnp.pad(index[None], ((0, 7), (0, 128 - 2 * held)))
    left = left_blocks.reshape(2, CHUNKS, rows, order)
    bf16 = jnp.bfloat16
    dma = pltpu.SemaphoreType.DMA
    scratch = [
        pltpu.VMEM((8, 8 + 4 * (2 + (CHUNKS if q == 0 else 0)), rows, order), bf16)
        for q in range(CHUNKS)
    ]
    scratch += [
        pltpu.VMEM((4, held, order, order), bf16),
        pltpu.VMEM((4, 8, 128), jnp.int32),
        pltpu.SMEM((4, 8, 128), jnp.int32),
        pltpu.VMEM((order, order), bf16),
        pltpu.VMEM((CHUNKS, 3, held, rows, order), bf16),
        pltpu.VMEM((held, rows, order), jnp.float32),
        pltpu.VMEM((CHUNKS, 2, held, rows, order), bf16),
        pltpu.VMEM((CHUNKS, held, rows, order), bf16),
        dma((6 + 60 * CHUNKS,)),
        dma((15 * CHUNKS,)),
        dma((CHUNKS, 8)),
        dma((CHUNKS, 2)),
        dma((CHUNKS, 8, 2)),
        dma((CHUNKS, 8)),
        dma((CHUNKS, 8, 3)),
        dma((4,)),
        dma((4,)),
        dma((CHUNKS, 3, 2)),
        dma((CHUNKS + 4,)),
    ]
    vmem, anywhere = pl.BlockSpec(memory_space=pltpu.VMEM), pl.BlockSpec(memory_space=pl.ANY)
    return pl.pallas_call(
        kernel,
        out_shape=jax.ShapeDtypeStruct(wavefunction.shape, wavefunction.dtype),
        in_specs=[anywhere, vmem, anywhere, anywhere],
        out_specs=vmem,
        scratch_shapes=scratch,
        compiler_params=pltpu.CompilerParams(
            collective_id=0, has_side_effects=True, vmem_limit_bytes=56 * 1024 * 1024),
        name="terms",
    )(wavefunction, index, left, right_blocks)


def solution(mesh):
    placed = (
        P(("term", "sector"), None, None),
        P(("term", "sector"), None),
        P(("term", "sector")),
        P("term", "sector", None, None),
        P("term", None, None, None),
    )
    return jax.shard_map(
        local,
        mesh=mesh,
        in_specs=placed,
        out_specs=P(("term", "sector"), None, None),
        check_vma=False,
    )
```

time: 390 us -> 70.9 us (0.18)
  waiting for transfers between devices: 159 us -> 0 us
  matrix products: 121 us -> 0 us
  Pallas kernels: 0 us -> 67.5 us
  local copies, waits for them, and re-layouts: 60.1 us -> 3.15 us
  starting transfers between devices: 38.8 us -> 0 us
  other arithmetic: 8.89 us -> 0.07 us
    ppermute x30 -> x0, waiting for transfers between devices: 125 us -> none  [from_behind(): return lax.ppermute(block, axis, route)]
    dot_general x32 -> x0, matrix products: 121 us -> none  [apply_terms(): jnp.einsum('kac,kdc->kad', mixed_left, chosen, preferred_element_type=jnp...]
    pallas_call x0 -> x1, Pallas kernels: none -> 67.5 us  [local(): pl.pallas_call(kernel, out_shape=jax.ShapeDtypeStruct(wavefunction.shape,...]
    gather x37 -> x0, local copies, waits for them, and re-layouts: 56.6 us -> none  [the longest x32 53.1 us: apply_terms(): chosen = jnp.take(right_now[index_term], slot_right, axis=0)]
    all_to_all x3 -> x0, starting transfers between devices: 35.4 us -> none  [the longest x1 22.3 us: local(): lax.all_to_all(out_slots, 'sector', split_axis=0, concat_axis=0, tiled=True)]
    all_to_all x3 -> x0, waiting for transfers between devices: 34.1 us -> none  [the longest x1 17.2 us: local(): lax.all_to_all(out_slots, 'sector', split_axis=0, concat_axis=0, tiled=True)]
  transfers between devices with their start and end apart: 33 -> 0, of which waited for: 18 -> 0; matrix products, arithmetic and copies ran while one was open for 2% -> 0% of each run, Pallas kernels for 0% -> 0%
where the time goes in v2:
time: 70.9 us; the launch traced here: 70.7 us
  Pallas kernels  67.5 us (95%)
  local copies, waits for them, and re-layouts  3.15 us (4%)
    pallas_call x1, Pallas kernels, local(): pl.pallas_call(kernel, out_shape=jax.ShapeDtypeStruct(wavefunction.shape,...  67.5 us
    unnamed x5, local copies, waits for them, and re-layouts  2.55 us

profile of v2, /device:TPU:1, one launch (start us, length us, event | category | flops | bytes accessed | tf_op | source)
XLA Modules:
  0.0 70.7 jit_solution(16642717596795448632)
XLA Ops:
  0.0 0.0 copy-start
  0.0 0.0 copy-start.1
  0.0 0.7 copy-done
  0.7 0.0 copy-done.1
  0.7 0.1 add_bitcast_fusion
  0.7 0.6 pad.4.i_in
  1.3 67.5 %terms.1 = bf16[16,128,128]{2,1,0:T(8,128)(2,1)} custom-call(bf16[16,128,128]{2,1,0:T(8,128)(2,1)} %x_in.1, s32[8,128]{1,0:T(8,128)} %pad.4.i_in, bf16[2,2,64,128]{3,2,1,0:T(8,128)(2,1)} %bitcast.4, bf16[2,4,128,128]{3,2,1,0:T(8,128)(2,1)} %r_in.1), custom_call_target="tpu_custom_call" | custom-call | tf_op jit(solution)/shard_map/terms/pallas_call | solution.py:327
  68.8 1.9 %copy.7 = bf16[16,128,128]{2,1,0:T(8,128)(2,1)} copy(bf16[16,128,128]{2,1,0:T(8,128)(2,1)} %terms.1) | data formatting | bytes 1048576
Async XLA Ops:
  0.0 0.7 copy-start
  0.0 0.7 copy-start.1

commit v3 on v2

--- a/solution.py
+++ b/solution.py
@@ -31,7 +31,8 @@
     h, x, c = sector // 8, lax.rem(sector // 2, 4), lax.rem(sector, 2)
     turn = 1 - 2 * c
     core = (term, sector + turn)
-    across = (lax.rem(term + 8, 16), sector)
+    across = ((lax.rem(term + 8, 16), sector),
+              (lax.rem(term + 8, 16), lax.rem(sector + 8, 16)))
 
     def z_at(k):
         return lax.rem(z + 16 + k * turn, 8)
@@ -54,14 +55,11 @@
     def b_at(q, xx):
         return 8 + xx * width(q)
 
-    def item(e):
-        return z_at(-e) if e <= 4 else z_at(e - 4)
-
     def a_half(q, e, half):
-        return W[q].at[item(e), pl.ds(4 * half, 4)]
+        return W[q].at[e, pl.ds(4 * half, 4)]
 
     def b_item(q, e, xx):
-        return W[q].at[item(e), pl.ds(b_at(q, xx), width(q))]
+        return W[q].at[e, pl.ds(b_at(q, xx), width(q))]
 
     right_own = pltpu.make_async_copy(r_in.at[c, x], r_own, loc_sem.at[0])
     right_own.start()
@@ -71,7 +69,7 @@
     keep_x.start()
 
     barrier = pltpu.get_barrier_semaphore()
-    peers = [across, z_dev(1), z_dev(-1), core]
+    peers = [*across, z_dev(1), z_dev(-1), core]
     for dh in range(2):
         for dx in range(4):
             if dh or dx:
@@ -82,7 +80,7 @@
     right_own.wait()
     turned = r_own[...].T
     for i in range(chunks):
-        W[0][z, b_at(0, x) + 2 + i] = turned[i * rows:(i + 1) * rows]
+        W[0][0, b_at(0, x) + 2 + i] = turned[i * rows:(i + 1) * rows]
 
     pl.semaphore_wait(barrier, len(peers))
 
@@ -103,7 +101,7 @@
 
     def own_copy(q):
         slot = jnp.where(c == 0, 2 * x + h, b_at(q, x) + h)
-        return pltpu.make_async_copy(l_in.at[c, q], W[q].at[z, slot], loc_sem.at[3 + q])
+        return pltpu.make_async_copy(l_in.at[c, q], W[q].at[0, slot], loc_sem.at[3 + q])
 
     for q in range(chunks):
         own_copy(q).start()
@@ -111,18 +109,18 @@
         @pl.when(c == 1)
         def _():
             slot = b_at(q, x) + h
-            send(l_in.at[0, q], W[q].at[z, slot], b_sem.at[q, 0], core, head1)
+            send(l_in.at[0, q], W[q].at[0, slot], b_sem.at[q, 0], core, head1)
             for j in range(2):
-                send(l_in.at[j, q], W[q].at[z, slot], b_sem.at[q, 1], plane(1, 0, j), head1)
+                send(l_in.at[j, q], W[q].at[0, slot], b_sem.at[q, 1], plane(1, 0, j), head1)
 
         @pl.when(c == 0)
         def _():
             slot = 2 * x + h
             for dh, dx in ((1, 2), (0, 2), (1, 1), (1, 3), (1, 0), (0, 1), (0, 3)):
                 for j in range(2):
-                    send(l_in.at[j, q], W[q].at[z, slot], a_sem.at[q, dh * 4 + dx],
+                    send(l_in.at[j, q], W[q].at[0, slot], a_sem.at[q, dh * 4 + dx],
                          plane(dh, dx, j), head0)
-            send(l_in.at[1, q], W[q].at[z, slot], a_sem.at[q, 0], core, head0)
+            send(l_in.at[1, q], W[q].at[0, slot], a_sem.at[q, 0], core, head0)
 
     def x_sends(q, e):
         mine = b_item(q, e, x)
@@ -132,15 +130,15 @@
     def column_ready(q):
         @pl.when(c == 0)
         def _():
-            arrived(W[q].at[z, b_at(q, x) + h], b_sem.at[q, 0])
+            arrived(W[q].at[0, b_at(q, x) + h], b_sem.at[q, 0])
 
         @pl.when(c == 1)
         def _():
             own_copy(q).wait()
-        arrived(W[q].at[z, b_at(q, x) + 1 - h], b_sem.at[q, 1])
+        arrived(W[q].at[0, b_at(q, x) + 1 - h], b_sem.at[q, 1])
         mine = b_item(q, 0, x)
-        send(mine, mine, bz_sem.at[q, 1], z_dev(1))
-        send(mine, mine, bz_sem.at[q, 5], z_dev(-1))
+        send(mine, b_item(q, 1, x), bz_sem.at[q, 1], z_dev(1))
+        send(mine, b_item(q, 5, x), bz_sem.at[q, 5], z_dev(-1))
         x_sends(q, 0)
 
     def row_ready(q):
@@ -150,16 +148,16 @@
 
         @pl.when(c == 1)
         def _():
-            arrived(W[q].at[z, 2 * x + h], a_sem.at[q, 0])
+            arrived(W[q].at[0, 2 * x + h], a_sem.at[q, 0])
         for dh in range(2):
             for dx in range(4):
                 if dh or dx:
                     slot = 2 * lax.rem(x + 4 - dx, 4) + lax.rem(h + dh, 2)
-                    arrived(W[q].at[z, slot], a_sem.at[q, dh * 4 + dx])
+                    arrived(W[q].at[0, slot], a_sem.at[q, dh * 4 + dx])
         for half in range(2):
             row = a_half(q, 0, half)
-            send(row, row, az_sem.at[q, 1, half], z_dev(1))
-            send(row, row, az_sem.at[q, 5, half], z_dev(-1))
+            send(row, a_half(q, 1, half), az_sem.at[q, 1, half], z_dev(1))
+            send(row, a_half(q, 5, half), az_sem.at[q, 5, half], z_dev(-1))
 
     def ways(d):
         return [w for w in ((d, 4, 1), (4 + d, 7, -1)) if w[0] <= w[1]]
@@ -170,14 +168,14 @@
                 row = a_half(q, e, half)
                 arrived(row, az_sem.at[q, e, half])
                 if e < last:
-                    send(row, row, az_sem.at[q, e + 1, half], z_dev(way))
+                    send(row, a_half(q, e + 1, half), az_sem.at[q, e + 1, half], z_dev(way))
 
     def tick_b(q, d):
         for e, last, way in ways(d):
             mine = b_item(q, e, x)
             arrived(mine, bz_sem.at[q, e])
             if e < last:
-                send(mine, mine, bz_sem.at[q, e + 1], z_dev(way))
+                send(mine, b_item(q, e + 1, x), bz_sem.at[q, e + 1], z_dev(way))
             x_sends(q, e)
 
     def tick_x(q, d):
@@ -193,39 +191,52 @@
 
     def exchange():
         send(i_in, i_all.at[1], i_sem.at[1], core)
-        send(i_in, i_all.at[2], i_sem.at[2], across)
         send(x_in, x_all.at[1], x_sem.at[1], core)
-        send(x_in, x_all.at[2], x_sem.at[2], across)
+        for side in range(2):
+            span = pl.ds(side * PIECE, PIECE)
+            send(i_in, i_all.at[2 + 2 * side], i_sem.at[2 + 2 * side], across[side])
+            send(x_in.at[span], x_all.at[2, span], x_sem.at[2 + 2 * side], across[side])
 
     def others():
         arrived(i_all.at[1], i_sem.at[1])
-        arrived(i_all.at[2], i_sem.at[2])
-        send(i_all.at[2], i_all.at[3], i_sem.at[3], core)
-        arrived(x_all.at[2], x_sem.at[2])
-        send(x_all.at[2], x_all.at[3], x_sem.at[3], core)
+        for side in range(2):
+            span = pl.ds(side * PIECE, PIECE)
+            got, passed = 2 + 2 * side, 3 + 2 * side
+            arrived(i_all.at[got], i_sem.at[got])
+            send(i_all.at[got], i_all.at[passed], i_sem.at[passed], core)
+            arrived(x_all.at[2, span], x_sem.at[got])
+            send(x_all.at[2, span], x_all.at[3, span], x_sem.at[passed], core)
         arrived(x_all.at[1], x_sem.at[1])
         keep.wait()
         keep_x.wait()
         arrived(i_all.at[3], i_sem.at[3])
+        arrived(i_all.at[5], i_sem.at[5])
         table = pltpu.make_async_copy(i_all, i_smem, loc_sem.at[3 + chunks])
         table.start()
-        arrived(x_all.at[3], x_sem.at[3])
+        for side in range(2):
+            span = pl.ds(side * PIECE, PIECE)
+            arrived(x_all.at[3, span], x_sem.at[3 + 2 * side])
         table.wait()
 
     def products(q, group, first, store):
-        for u in range(PIECE):
-            k = first + u
-            left, right = i_smem[group, 0, k], i_smem[group, 0, held + k]
+        terms = range(8)
+        many = len(terms)
+        halves = []
+        for k in range(first, first + PIECE):
+            table = group + 2 if group >= 2 and k >= PIECE else group
+            left = i_smem[table, 0, k]
             spot, half, odd = (left >> 1) & 3, left >> 3, left & 1
             slot = jnp.where(odd == 0, 2 * spot + half, b_at(q, spot) + half)
-            tall = jnp.concatenate([W[q][e, slot] for e in range(8)], axis=0)
-            mixed = jnp.dot(
+            tall = jnp.concatenate([W[q][e, slot] for e in terms], axis=0)
+            halves.append(jnp.dot(
                 tall, x_all[group, k], preferred_element_type=jnp.float32
-            ).astype(jnp.bfloat16)
-            wide = jnp.concatenate([mixed[e * rows:(e + 1) * rows] for e in range(8)], axis=1)
-            at = b_at(0, right) + 2
+            ).astype(jnp.bfloat16))
+        for k, mixed in zip(range(first, first + PIECE), halves):
+            table = group + 2 if group >= 2 and k >= PIECE else group
+            wide = jnp.concatenate([mixed[e * rows:(e + 1) * rows] for e in range(many)], axis=1)
+            at = b_at(0, i_smem[table, 0, held + k]) + 2
             chosen = jnp.concatenate(
-                [W[0][e, at + i] for e in range(8) for i in range(chunks)], axis=0)
+                [W[0][e, at + i] for e in terms for i in range(chunks)], axis=0)
             store(k, jnp.dot(wide, chosen, preferred_element_type=jnp.float32))
 
     def piece(q, number):
@@ -245,7 +256,8 @@
             arrived(got_core.at[q, 0, span], red_sem.at[q, 0, number % 2])
             part[q, 1, span] = (
                 acc[span] + got_core[q, 0, span].astype(jnp.float32)).astype(jnp.bfloat16)
-            send(part.at[q, 1, span], got_y.at[q, span], red_sem.at[q, 1, number % 2], across)
+            send(part.at[q, 1, span], got_y.at[q, span], red_sem.at[q, 1, number % 2],
+                 across[number % 2])
         if stage == 2:
             products(q, 1, first, to_part)
             send(part.at[q, 2, span], got_core.at[q, 1, span], red_sem.at[q, 2, number % 2], core)
@@ -304,22 +316,22 @@
     ]
     scratch += [
         pltpu.VMEM((4, held, order, order), bf16),
-        pltpu.VMEM((4, 8, 128), jnp.int32),
-        pltpu.SMEM((4, 8, 128), jnp.int32),
+        pltpu.VMEM((6, 8, 128), jnp.int32),
+        pltpu.SMEM((6, 8, 128), jnp.int32),
         pltpu.VMEM((order, order), bf16),
         pltpu.VMEM((CHUNKS, 3, held, rows, order), bf16),
         pltpu.VMEM((held, rows, order), jnp.float32),
         pltpu.VMEM((CHUNKS, 2, held, rows, order), bf16),
         pltpu.VMEM((CHUNKS, held, rows, order), bf16),
-        dma((6 + 60 * CHUNKS,)),
+        dma((12 + 60 * CHUNKS,)),
         dma((15 * CHUNKS,)),
         dma((CHUNKS, 8)),
         dma((CHUNKS, 2)),
         dma((CHUNKS, 8, 2)),
         dma((CHUNKS, 8)),
         dma((CHUNKS, 8, 3)),
-        dma((4,)),
-        dma((4,)),
+        dma((6,)),
+        dma((6,)),
         dma((CHUNKS, 3, 2)),
         dma((CHUNKS + 4,)),
     ]

time: 70.9 us -> 69.5 us (0.980)
  Pallas kernels: 67.5 us -> 66.1 us
    pallas_call x1, Pallas kernels: 67.5 us -> 66.1 us  [local(): pl.pallas_call(kernel, out_shape=jax.ShapeDtypeStruct(wavefunction.shape,...]
where the time goes in v3:
time: 69.5 us; the launch traced here: 69.3 us
  Pallas kernels  66.1 us (95%)
  local copies, waits for them, and re-layouts  3.15 us (5%)
    pallas_call x1, Pallas kernels, local(): pl.pallas_call(kernel, out_shape=jax.ShapeDtypeStruct(wavefunction.shape,...  66.1 us
    unnamed x5, local copies, waits for them, and re-layouts  2.55 us

profile of v3, /device:TPU:1, one launch (start us, length us, event | category | flops | bytes accessed | tf_op | source)
XLA Modules:
  0.0 69.3 jit_solution(2458089346471724835)
XLA Ops:
  0.0 0.0 copy-start
  0.0 0.0 copy-start.1
  0.0 0.7 copy-done
  0.7 0.0 copy-done.1
  0.7 0.1 add_bitcast_fusion
  0.7 0.6 pad.4.i_in
  1.3 66.1 %terms.1 = bf16[16,128,128]{2,1,0:T(8,128)(2,1)} custom-call(bf16[16,128,128]{2,1,0:T(8,128)(2,1)} %x_in.1, s32[8,128]{1,0:T(8,128)} %pad.4.i_in, bf16[2,2,64,128]{3,2,1,0:T(8,128)(2,1)} %bitcast.4, bf16[2,4,128,128]{3,2,1,0:T(8,128)(2,1)} %r_in.1), custom_call_target="tpu_custom_call" | custom-call | tf_op jit(solution)/shard_map/terms/pallas_call | solution.py:339
  67.4 1.9 %copy.7 = bf16[16,128,128]{2,1,0:T(8,128)(2,1)} copy(bf16[16,128,128]{2,1,0:T(8,128)(2,1)} %terms.1) | data formatting | bytes 1048576
Async XLA Ops:
  0.0 0.7 copy-start
  0.0 0.7 copy-start.1

commit v4 on v3

--- a/solution.py
+++ b/solution.py
@@ -11,10 +11,11 @@
 PIECE = 8
 MESH = pl.DeviceIdType.MESH
 ORDER = (
-    "0R", "1R", "0r", "0B1", "0X0", "0A1", "1r", "0B2", "0X1", "0A2", "0B3", "0X2", "0A3",
-    "0B4", "0X3", "0A4", "1B1", "1X0", "1A1", "0X4", "1B2", "1X1", "1A2", "0C", "O", "0P0",
-    "0P1", "1B3", "1X2", "1A3", "0P2", "0P3", "1B4", "1X3", "1A4", "0P4", "0P5", "1X4", "0P6",
-    "0P7", "1C", "1P0", "1P1", "1P2", "1P3", "1P4", "1P5", "1P6", "1P7",
+    "0R", "1R", "0r", "0B1", "0X0", "0A1", "0B2", "0X1", "0A2", "1r", "0B3", "0X2", "0A3", "o",
+    "0B4", "0X3", "1B1", "1X0", "1A1", "0X4", "1B2", "1X1", "1A2", "0A4", "0K0", "0K1", "0K2",
+    "0K3", "0K4", "O", "0P0", "1B3", "1X2", "1A3", "0P1", "0P2", "1B4", "0P3", "1X3", "0P4",
+    "1X4", "0P5", "0P6", "0P7", "1A4", "1K0", "1K1", "1K2", "1K3", "1K4", "1P0", "1P1", "1P2",
+    "1P3", "1P4", "1P5", "1P6", "1P7",
 )
 
 
@@ -179,13 +180,16 @@
             x_sends(q, e)
 
     def tick_x(q, d):
-        for e in ((0,) if d == 0 else [w[0] for w in ways(d)]):
+        for e in items(d):
             passed = b_item(q, e, x_at(-1))
             arrived(passed, bx_sem.at[q, e, 0])
             send(passed, passed, bx_sem.at[q, e, 2], x_dev(1))
 
-    def closing(q):
-        for e in range(8):
+    def items(d):
+        return (0,) if d == 0 else [w[0] for w in ways(d)]
+
+    def tick_k(q, d):
+        for e in items(d):
             arrived(b_item(q, e, x_at(1)), bx_sem.at[q, e, 1])
             arrived(b_item(q, e, x_at(2)), bx_sem.at[q, e, 2])
 
@@ -198,7 +202,6 @@
             send(x_in.at[span], x_all.at[2, span], x_sem.at[2 + 2 * side], across[side])
 
     def others():
-        arrived(i_all.at[1], i_sem.at[1])
         for side in range(2):
             span = pl.ds(side * PIECE, PIECE)
             got, passed = 2 + 2 * side, 3 + 2 * side
@@ -206,6 +209,9 @@
             send(i_all.at[got], i_all.at[passed], i_sem.at[passed], core)
             arrived(x_all.at[2, span], x_sem.at[got])
             send(x_all.at[2, span], x_all.at[3, span], x_sem.at[passed], core)
+
+    def ready():
+        arrived(i_all.at[1], i_sem.at[1])
         arrived(x_all.at[1], x_sem.at[1])
         keep.wait()
         keep_x.wait()
@@ -240,38 +246,39 @@
             store(k, jnp.dot(wide, chosen, preferred_element_type=jnp.float32))
 
     def piece(q, number):
-        stage, first = number // 2, (number % 2) * PIECE
-        span = pl.ds(first, PIECE)
+        finish(q, number // 2, (number % 2,))
+
+    def finish(q, stage, sides):
+        group = 3 - stage
 
         def to_part(k, value):
             part[q, stage, k] = value.astype(jnp.bfloat16)
 
         def to_acc(k, value):
             acc[k] = value
-        if stage == 0:
-            products(q, 3, first, to_part)
-            send(part.at[q, 0, span], got_core.at[q, 0, span], red_sem.at[q, 0, number % 2], core)
-        if stage == 1:
-            products(q, 2, first, to_acc)
-            arrived(got_core.at[q, 0, span], red_sem.at[q, 0, number % 2])
-            part[q, 1, span] = (
-                acc[span] + got_core[q, 0, span].astype(jnp.float32)).astype(jnp.bfloat16)
-            send(part.at[q, 1, span], got_y.at[q, span], red_sem.at[q, 1, number % 2],
-                 across[number % 2])
-        if stage == 2:
-            products(q, 1, first, to_part)
-            send(part.at[q, 2, span], got_core.at[q, 1, span], red_sem.at[q, 2, number % 2], core)
-        if stage == 3:
-            products(q, 0, first, to_acc)
-            arrived(got_core.at[q, 1, span], red_sem.at[q, 2, number % 2])
-            arrived(got_y.at[q, span], red_sem.at[q, 1, number % 2])
-            total = (acc[span] + got_core[q, 1, span].astype(jnp.float32)
-                     + got_y[q, span].astype(jnp.float32))
-            o_ref[span, pl.ds(q * rows, rows)] = total.astype(jnp.bfloat16)
+        for side in sides:
+            products(q, group, side * PIECE, to_acc if stage % 2 else to_part)
+        for side in sides:
+            span = pl.ds(side * PIECE, PIECE)
+            if stage == 0:
+                send(part.at[q, 0, span], got_core.at[q, 0, span], red_sem.at[q, 0, side], core)
+            if stage == 1:
+                arrived(got_core.at[q, 0, span], red_sem.at[q, 0, side])
+                part[q, 1, span] = (
+                    acc[span] + got_core[q, 0, span].astype(jnp.float32)).astype(jnp.bfloat16)
+                send(part.at[q, 1, span], got_y.at[q, span], red_sem.at[q, 1, side], across[side])
+            if stage == 2:
+                send(part.at[q, 2, span], got_core.at[q, 1, span], red_sem.at[q, 2, side], core)
+            if stage == 3:
+                arrived(got_core.at[q, 1, span], red_sem.at[q, 2, side])
+                arrived(got_y.at[q, span], red_sem.at[q, 1, side])
+                total = (acc[span] + got_core[q, 1, span].astype(jnp.float32)
+                         + got_y[q, span].astype(jnp.float32))
+                o_ref[span, pl.ds(q * rows, rows)] = total.astype(jnp.bfloat16)
 
     for name in ORDER:
-        if name == "O":
-            others()
+        if name in ("o", "O"):
+            (others if name == "o" else ready)()
             continue
         q, what, d = int(name[0]), name[1], int(name[2:] or 0)
         if what == "R":
@@ -286,8 +293,10 @@
             tick_b(q, d)
         if what == "X":
             tick_x(q, d)
-        if what == "C":
-            closing(q)
+        if what == "K":
+            tick_k(q, d)
+        if what == "S":
+            finish(q, d, (0, 1))
         if what == "P":
             piece(q, d)
 

time: 69.5 us -> 67.2 us (0.967)
  Pallas kernels: 66.1 us -> 63.8 us
    pallas_call x1, Pallas kernels: 66.1 us -> 63.8 us  [local(): pl.pallas_call(kernel, out_shape=jax.ShapeDtypeStruct(wavefunction.shape,...]
where the time goes in v4:
time: 67.2 us; the launch traced here: 67 us
  Pallas kernels  63.8 us (95%)
  local copies, waits for them, and re-layouts  3.15 us (5%)
    pallas_call x1, Pallas kernels, local(): pl.pallas_call(kernel, out_shape=jax.ShapeDtypeStruct(wavefunction.shape,...  63.8 us
    unnamed x5, local copies, waits for them, and re-layouts  2.55 us

profile of v4, /device:TPU:1, one launch (start us, length us, event | category | flops | bytes accessed | tf_op | source)
XLA Modules:
  0.0 67.0 jit_solution(12499427310374929727)
XLA Ops:
  0.0 0.0 copy-start
  0.0 0.0 copy-start.1
  0.0 0.7 copy-done
  0.7 0.0 copy-done.1
  0.7 0.1 add_bitcast_fusion
  0.7 0.6 pad.4.i_in
  1.3 63.8 %terms.1 = bf16[16,128,128]{2,1,0:T(8,128)(2,1)} custom-call(bf16[16,128,128]{2,1,0:T(8,128)(2,1)} %x_in.1, s32[8,128]{1,0:T(8,128)} %pad.4.i_in, bf16[2,2,64,128]{3,2,1,0:T(8,128)(2,1)} %bitcast.4, bf16[2,4,128,128]{3,2,1,0:T(8,128)(2,1)} %r_in.1), custom_call_target="tpu_custom_call" | custom-call | tf_op jit(solution)/shard_map/terms/pallas_call | solution.py:348
  65.1 1.9 %copy.7 = bf16[16,128,128]{2,1,0:T(8,128)(2,1)} copy(bf16[16,128,128]{2,1,0:T(8,128)(2,1)} %terms.1) | data formatting | bytes 1048576
Async XLA Ops:
  0.0 0.7 copy-start
  0.0 0.7 copy-start.1

commit v5 on v4

--- a/solution.py
+++ b/solution.py
@@ -11,9 +11,9 @@
 PIECE = 8
 MESH = pl.DeviceIdType.MESH
 ORDER = (
-    "0R", "1R", "0r", "0B1", "0X0", "0A1", "0B2", "0X1", "0A2", "1r", "0B3", "0X2", "0A3", "o",
-    "0B4", "0X3", "1B1", "1X0", "1A1", "0X4", "1B2", "1X1", "1A2", "0A4", "0K0", "0K1", "0K2",
-    "0K3", "0K4", "O", "0P0", "1B3", "1X2", "1A3", "0P1", "0P2", "1B4", "0P3", "1X3", "0P4",
+    "0R", "1R", "0r", "0B1", "0X0", "0A1", "0B2", "0X1", "0A2", "1r", "0B3", "0X2", "0B4", "o",
+    "0A3", "0X3", "1B1", "1X0", "1A1", "0X4", "1B2", "1X1", "1A2", "1B3", "0A4", "0K0", "0K1",
+    "0K2", "0K3", "0K4", "O", "0P0", "1X2", "1A3", "0P1", "0P2", "1B4", "0P3", "1X3", "0P4",
     "1X4", "0P5", "0P6", "0P7", "1A4", "1K0", "1K1", "1K2", "1K3", "1K4", "1P0", "1P1", "1P2",
     "1P3", "1P4", "1P5", "1P6", "1P7",
 )

time: 67.2 us -> 67.3 us (level)
  no operation moved by 1% of the time
where the time goes in v5:
time: 67.3 us; the launch traced here: 67 us
  Pallas kernels  63.8 us (95%)
  local copies, waits for them, and re-layouts  3.15 us (5%)
    pallas_call x1, Pallas kernels, local(): pl.pallas_call(kernel, out_shape=jax.ShapeDtypeStruct(wavefunction.shape,...  63.8 us
    unnamed x5, local copies, waits for them, and re-layouts  2.55 us

profile of v5, /device:TPU:1, one launch (start us, length us, event | category | flops | bytes accessed | tf_op | source)
XLA Modules:
  0.0 67.0 jit_solution(3587526414886702544)
XLA Ops:
  0.0 0.0 copy-start
  0.0 0.0 copy-start.1
  0.0 0.7 copy-done
  0.7 0.0 copy-done.1
  0.7 0.1 add_bitcast_fusion
  0.7 0.6 pad.4.i_in
  1.3 63.8 %terms.1 = bf16[16,128,128]{2,1,0:T(8,128)(2,1)} custom-call(bf16[16,128,128]{2,1,0:T(8,128)(2,1)} %x_in.1, s32[8,128]{1,0:T(8,128)} %pad.4.i_in, bf16[2,2,64,128]{3,2,1,0:T(8,128)(2,1)} %bitcast.4, bf16[2,4,128,128]{3,2,1,0:T(8,128)(2,1)} %r_in.1), custom_call_target="tpu_custom_call" | custom-call | tf_op jit(solution)/shard_map/terms/pallas_call | solution.py:348
  65.2 1.9 %copy.7 = bf16[16,128,128]{2,1,0:T(8,128)(2,1)} copy(bf16[16,128,128]{2,1,0:T(8,128)(2,1)} %terms.1) | data formatting | bytes 1048576
Async XLA Ops:
  0.0 0.7 copy-start
  0.0 0.7 copy-start.1
